TPU v7x, 128 devices: a whole 4x4x4 slice. The times are simulated.
128 devices in a mesh: row: 8 (over x, y_hi), col: 16 (over z, y_lo, core).
Axes of the slice: x: 4, y: 4 (y_hi: 2, y_lo: 2; y = y_hi * 2 + y_lo), z: 4, core: 2. Of those that a mesh axis runs over, the one named last changes fastest.
Arguments:
- latent: bfloat16 [128, 128, 256], P('row', 'col'), may hold values from -6 to 6
- well_logs: bfloat16 [128, 256], P(('row', 'col')), may hold values from -6 to 6
- cond_weight: bfloat16 [256, 256], replicated, may hold values from -0.375 to 0.375
- trace_rows: int32 [128], P('col'), may hold values from 0 to 127, as said below
- norm_gain: float32 [256], replicated, may hold values from 0.5 to 1.5
- in_weight: bfloat16 [256, 512], replicated, may hold values from -0.375 to 0.375
- conv_weight: float32 [9, 256], replicated, may hold values from -2 to 2
- bc_weight: bfloat16 [256, 1024], replicated, may hold values from -0.375 to 0.375
- dt_weight: bfloat16 [256, 64], replicated, may hold values from -0.375 to 0.375
- dt_bias: float32 [4, 16], replicated, may hold values from -0.5 to 0.5
- row_rate: float32 [2, 16], replicated, may hold values from 1 to 512
- col_rate: float32 [2, 16], replicated, may hold values from 1 to 512
- horizon: float32 [128, 128], P('row', 'col'), may hold values from 0 to 1
- out_gain: float32 [256], replicated, may hold values from 0.5 to 1.5
- out_weight: bfloat16 [256, 256], replicated, may hold values from -0.375 to 0.375
Outputs:
- block_out: bfloat16 [128, 128, 256], P('row', 'col')
Inputs may be any that keep to these rules, and one draw needn't show every extreme that they name: `trace_rows`: every conditioning token row is named by some plane column.
All inputs are finite; a program needn't handle non-finite values.
Results may differ from a plain program's by a relative error of at most 0.009.
Values may be sent and summed in bfloat16 or wider, within the bound.
No kernel may reach another device: no remote copies, remote signals or barrier semaphores. Data moves between devices by JAX's collectives and lax.ppermute only.
A program may use at most 192 MiB of HBM per device.

v0:
```python
import jax
import jax.numpy as jnp
from jax import lax
from jax.sharding import PartitionSpec as P

precise = lax.Precision.HIGHEST


def padded_2(cells, sides, width):
    for axis, dim in sides:
        count = lax.axis_size(axis)
        ends = count - 1
        head = lax.slice_in_dim(cells, 0, width, axis=dim)
        tail = lax.slice_in_dim(cells, cells.shape[dim] - width, cells.shape[dim], axis=dim)
        cells = jnp.concatenate(
            [
                lax.ppermute(tail, axis, [(i, (i + 1) % count) for i in range(ends)]),
                cells,
                lax.ppermute(head, axis, [((i + 1) % count, i) for i in range(ends)]),
            ],
            axis=dim,
        )
    return cells


def entering(array, axis, join, neutral, backward):
    count = lax.axis_size(axis)
    place = lax.axis_index(axis)
    ahead = count - 1 - place if backward else place
    gathered = jax.tree.map(
        lambda a, kind: lax.all_gather(a.astype(kind), axis), array, (jnp.bfloat16, jnp.bfloat16)
    )
    state = jax.tree.map(lambda a, e: jnp.zeros_like(a) + jnp.asarray(e, a.dtype), array, neutral)

    def one(turn, state):
        source = count - 1 - turn if backward else turn
        return join(
            state,
            jax.tree.map(
                lambda a, own: lax.dynamic_index_in_dim(a, source, 0, False).astype(own.dtype),
                gathered,
                array,
            ),
        )

    return lax.fori_loop(0, ahead, one, state)


def segment_recurrence(states, pieces):
    signal, in_coef, out_coef, step_size, log_decay = pieces
    block_len = signal.shape[1]
    cumulative = jnp.cumsum(log_decay, axis=1)
    scores = jnp.einsum("lks,ljs->lkj", out_coef, in_coef, preferred_element_type=jnp.float32)
    driven = signal.astype(jnp.float32) * step_size[..., None]
    causal = jnp.arange(block_len)[:, None] >= jnp.arange(block_len)[None, :]

    def head_term(head_args):
        head_cum, head_drive = head_args
        spread = jnp.where(causal, head_cum[:, :, None] - head_cum[:, None, :], -jnp.inf)
        return jnp.einsum("lkj,ljp->lkp", scores * jnp.exp(spread), head_drive, precision=precise)

    inner = lax.map(head_term, (jnp.moveaxis(cumulative, 2, 0), jnp.moveaxis(driven, 2, 0)))
    inner = jnp.moveaxis(inner, 0, 2)
    carried_in = jnp.exp(cumulative)[..., None] * jnp.einsum(
        "lks,lhps->lkhp", out_coef.astype(jnp.float32), states, precision=precise
    )
    tail_decay = jnp.exp(cumulative[:, -1:, :] - cumulative)
    states = jnp.exp(cumulative[:, -1, :])[:, :, None, None] * states + jnp.einsum(
        "lkhp,lks->lhps",
        driven * tail_decay[..., None],
        in_coef.astype(jnp.float32),
        precision=precise,
    )
    output = inner + carried_in
    return (states, output.reshape(output.shape[0], block_len, -1))


def line_scan(signal, in_coef, out_coef, step_size, log_decay, states):
    line_count = signal.shape[0]
    length = signal.shape[1]
    block_len = min(64, length)
    blocks = length // block_len

    def split_blocks(array):
        shaped = array.reshape((line_count, blocks, block_len) + array.shape[2:])
        return jnp.moveaxis(shaped, 1, 0)

    pieces = (
        split_blocks(signal),
        split_blocks(in_coef),
        split_blocks(out_coef),
        split_blocks(step_size),
        split_blocks(log_decay),
    )
    states, outputs = lax.scan(segment_recurrence, states, pieces)
    outputs = jnp.moveaxis(outputs, 0, 1).reshape(line_count, length, -1)
    return (outputs, states)


def orient(array, along_columns, backward):
    if along_columns:
        array = jnp.swapaxes(array, 0, 1)
    if backward:
        array = jnp.flip(array, 1)
    return array


def restore(array, along_columns, backward):
    if backward:
        array = jnp.flip(array, 1)
    if along_columns:
        array = jnp.swapaxes(array, 0, 1)
    return array


def direction_inputs(mixed, marks, bc_weight, dt_weight, dt_bias, rate_row, line_length, direction):
    tile_shape = mixed.shape[:2]
    inner_width = mixed.shape[2]
    head_count = dt_bias.shape[1]
    state_dim = bc_weight.shape[1] // 8
    flat_x = mixed.reshape(-1, inner_width)
    coef_pair = (
        jnp.dot(
            flat_x,
            bc_weight[:, direction * 2 * state_dim : (direction + 1) * 2 * state_dim],
            preferred_element_type=jnp.float32,
        )
        .astype(jnp.bfloat16)
        .reshape(tile_shape + (2 * state_dim,))
    )
    step_size = jax.nn.softplus(
        jnp.dot(
            flat_x,
            dt_weight[:, direction * head_count : (direction + 1) * head_count],
            preferred_element_type=jnp.float32,
        ).reshape(tile_shape + (head_count,))
        + dt_bias[direction]
    )
    log_decay = -step_size * (rate_row / (16.0 * line_length)) - marks[:, :, None]
    signal = mixed.reshape(tile_shape + (head_count, inner_width // head_count))
    return (signal, coef_pair[..., :state_dim], coef_pair[..., state_dim:], step_size, log_decay)


def oriented_scan(inputs, along_columns, backward):
    signal_l = orient(inputs[0], along_columns, backward)
    in_l = orient(inputs[1], along_columns, backward)
    out_l = orient(inputs[2], along_columns, backward)
    step_l = orient(inputs[3], along_columns, backward)
    decay_l = orient(inputs[4], along_columns, backward)
    zero_states = jnp.zeros(
        (signal_l.shape[0], signal_l.shape[2], signal_l.shape[3], in_l.shape[2]), jnp.float32
    )
    outputs, states = line_scan(signal_l, in_l, out_l, step_l, decay_l, zero_states)
    cumulative = jnp.cumsum(decay_l, axis=1)
    return (outputs, states, jnp.exp(cumulative[:, -1, :]), cumulative, out_l)


def finish(outputs, cumulative, out_l, inflow, along_columns, backward):
    extra = jnp.exp(cumulative)[..., None] * jnp.einsum(
        "lks,lhps->lkhp", out_l.astype(jnp.float32), inflow, precision=precise
    )
    return restore(outputs + extra.reshape(outputs.shape), along_columns, backward)


def combine_states(earlier, later):
    return (earlier[0] * later[0], later[0][:, :, None, None] * earlier[1] + later[1])


def per_device(
    latent,
    well_logs,
    cond_weight,
    trace_rows,
    norm_gain,
    in_weight,
    conv_weight,
    bc_weight,
    dt_weight,
    dt_bias,
    row_rate,
    col_rate,
    horizon,
    out_gain,
    out_weight,
):
    tile_rows, tile_cols, width = latent.shape
    inner_width = in_weight.shape[1] // 2
    row_length = tile_cols * lax.axis_size("col")
    col_length = tile_rows * lax.axis_size("row")
    local_tokens = jax.nn.silu(
        jnp.dot(well_logs, cond_weight, preferred_element_type=jnp.float32)
    ).astype(jnp.bfloat16)
    shard_rows = lax.all_gather(local_tokens, ("row", "col"), axis=0, tiled=True)
    positions = jnp.arange(shard_rows.shape[0])[None, :]
    select = (trace_rows[:, None] == positions).astype(jnp.bfloat16)
    column_tokens = jnp.dot(select, shard_rows, preferred_element_type=jnp.float32)
    hidden = latent.astype(jnp.float32) + column_tokens[None, :, :]
    normed = (
        hidden * lax.rsqrt(jnp.mean(hidden * hidden, axis=-1, keepdims=True) + 1e-06) * norm_gain
    ).astype(jnp.bfloat16)
    projected = (
        jnp.dot(normed.reshape(-1, width), in_weight, preferred_element_type=jnp.float32)
        .astype(jnp.bfloat16)
        .reshape(tile_rows, tile_cols, 2 * inner_width)
    )
    pre_conv = projected[..., :inner_width]
    gating_share = projected[..., inner_width:]
    padded = padded_2(pre_conv, (("row", 0), ("col", 1)), 1)
    conv_sum = jnp.zeros((tile_rows, tile_cols, inner_width), jnp.float32)
    for offset_row in range(3):
        for offset_col in range(3):
            conv_sum = (
                conv_sum
                + padded[
                    offset_row : offset_row + tile_rows, offset_col : offset_col + tile_cols
                ].astype(jnp.float32)
                * conv_weight[3 * offset_row + offset_col]
            )
    mixed_x = jax.nn.silu(conv_sum).astype(jnp.bfloat16)
    ahead = oriented_scan(
        direction_inputs(
            mixed_x, horizon, bc_weight, dt_weight, dt_bias, row_rate[0], row_length, 0
        ),
        False,
        False,
    )
    inflow_ahead = entering(
        (ahead[2], ahead[1]),
        "col",
        combine_states,
        (jnp.ones_like(ahead[2]), jnp.zeros_like(ahead[1])),
        False,
    )[1]
    behind = oriented_scan(
        direction_inputs(
            mixed_x, horizon, bc_weight, dt_weight, dt_bias, row_rate[1], row_length, 1
        ),
        False,
        True,
    )
    inflow_behind = entering(
        (behind[2], behind[1]),
        "col",
        combine_states,
        (jnp.ones_like(behind[2]), jnp.zeros_like(behind[1])),
        True,
    )[1]
    row_total = finish(ahead[0], ahead[3], ahead[4], inflow_ahead, False, False) + finish(
        behind[0], behind[3], behind[4], inflow_behind, False, True
    )
    ahead = oriented_scan(
        direction_inputs(
            mixed_x, horizon, bc_weight, dt_weight, dt_bias, col_rate[0], col_length, 2
        ),
        True,
        False,
    )
    inflow_ahead = entering(
        (ahead[2], ahead[1]),
        "row",
        combine_states,
        (jnp.ones_like(ahead[2]), jnp.zeros_like(ahead[1])),
        False,
    )[1]
    behind = oriented_scan(
        direction_inputs(
            mixed_x, horizon, bc_weight, dt_weight, dt_bias, col_rate[1], col_length, 3
        ),
        True,
        True,
    )
    inflow_behind = entering(
        (behind[2], behind[1]),
        "row",
        combine_states,
        (jnp.ones_like(behind[2]), jnp.zeros_like(behind[1])),
        True,
    )[1]
    col_total = finish(ahead[0], ahead[3], ahead[4], inflow_ahead, True, False) + finish(
        behind[0], behind[3], behind[4], inflow_behind, True, True
    )
    total = row_total + col_total
    gated = (
        total
        * lax.rsqrt(jnp.mean(total * total, axis=-1, keepdims=True) + 1e-05)
        * out_gain
        * jax.nn.silu(gating_share.astype(jnp.float32))
    ).astype(jnp.bfloat16)
    branch = jnp.dot(
        gated.reshape(-1, inner_width), out_weight, preferred_element_type=jnp.float32
    ).reshape(tile_rows, tile_cols, width)
    return (hidden + branch).astype(jnp.bfloat16)


def solution(mesh):
    placed = (
        P("row", "col", None),
        P(("row", "col"), None),
        P(),
        P("col"),
        P(),
        P(),
        P(),
        P(),
        P(),
        P(),
        P(),
        P(),
        P("row", "col"),
        P(),
        P(),
    )
    return jax.shard_map(
        per_device, mesh=mesh, in_specs=placed, out_specs=P("row", "col", None), check_vma=False
    )
```

profile of v0, /device:TPU:1, one launch (start us, length us, event | category | flops | bytes accessed | tf_op | source)
XLA Modules:
  0.0 588.6 jit_solution(4522145251670227212)
XLA Ops:
  7.7 180.3 %all-gather.9 = bf16[128,1,256]{2,1,0:T(2,128)(2,1)S(1)} all-gather(bf16[1,1,256]{2,1,0:T(2,128)(2,1)S(1)} %reshape.389), channel_id=2, replica_groups=mesh['row'=8,'col'=16] {'row','col'}, dimensions={0}, use_global_device_ids=true | all-gather | bytes 66048 | tf_op jit(solution)/shard_map/all_gather | solution.py:193
  192.2 5.5 collective-permute-start
  201.6 2.4 collective-permute-start.3
  209.5 2.2 fusion.56
  214.7 2.2 fusion.57
  220.4 3.0 add_convert_fusion.1
  227.8 26.5 %all-gather.5 = bf16[64,1,16]{2,0,1:T(8,128)(2,1)} all-gather(bf16[8,1,16]{2,0,1:T(8,128)(2,1)S(1)} %get-tuple-element.753), channel_id=7, replica_groups=mesh['row'=8,'col'=16] {'row'}, dimensions={0}, use_global_device_ids=true | all-gather | bytes 2304 | tf_op jit(solution)/shard_map/all_gather | solution.py:31
  254.3 26.0 %all-gather.7 = bf16[64,1,16]{2,0,1:T(8,128)(2,1)S(1)} all-gather(bf16[8,1,16]{2,0,1:T(8,128)(2,1)S(1)} %get-tuple-element.745), channel_id=9, replica_groups=mesh['row'=8,'col'=16] {'row'}, dimensions={0}, use_global_device_ids=true | all-gather | bytes 2304 | tf_op jit(solution)/shard_map/all_gather | solution.py:31
  280.3 25.5 %all-gather.1 = bf16[256,1,16]{2,0,1:T(8,128)(2,1)} all-gather(bf16[16,1,16]{2,0,1:T(8,128)(2,1)S(1)} %get-tuple-element.741), channel_id=3, replica_groups=mesh['row'=8,'col'=16] {'col'}, dimensions={0}, use_global_device_ids=true | all-gather | bytes 8704 | tf_op jit(solution)/shard_map/all_gather | solution.py:31
  305.8 18.3 %all-gather.3 = bf16[256,1,16]{2,0,1:T(8,128)(2,1)} all-gather(bf16[16,1,16]{2,0,1:T(8,128)(2,1)S(1)} %get-tuple-element.735), channel_id=5, replica_groups=mesh['row'=8,'col'=16] {'col'}, dimensions={0}, use_global_device_ids=true | all-gather | bytes 8704 | tf_op jit(solution)/shard_map/all_gather | solution.py:31
  325.0 3.0 add_convert_fusion
  328.0 6.2 %while.134 = (s32[]{:T(128)}, f32[16,8,16,16]{3,2,0,1:T(8,128)S(1)}, f32[16,8,16]{2,1,0:T(8,128)S(1)}, f32[8,16,16]{2,1,0:T(8,128)S(1)}, f32[16,8,16,16]{3,0,1,2:T(8,128)S(1)}, /*index=5*/s32[]{:T(128)}) while((s32[]{:T(128)}, f32[16,8,16,16]{3,2,0,1:T(8,128)S(1)}, f32[16,8,16]{2,1,0:T(8,128)S(1)}, f32[8,16,16]{2,1,0:T(8,128)S(1)}, ...), condition=%wide.region_13.14_spmd.clone, body=%wide.region_12.13_spmd.clone.sunk | while | flops 399618 | bytes 224601 | solution.py:62
  334.8 33.3 %while.135 = (s32[]{:T(128)}, f32[16,8,16,16]{3,2,0,1:T(8,128)S(1)}, f32[16,8,16]{2,1,0:T(8,128)}, f32[8,16,16]{2,1,0:T(8,128)S(1)}, f32[16,8,16,16]{3,0,1,2:T(8,128)}, /*index=5*/s32[]{:T(128)}) while((s32[]{:T(128)}, f32[16,8,16,16]{3,2,0,1:T(8,128)S(1)}, f32[16,8,16]{2,1,0:T(8,128)}, f32[8,16,16]{2,1,0:T(8,128)S(1)}, ...), condition=%wide.region_18.19_spmd.clone, body=%wide.region_17.18_spmd.clone.sunk | while | flops 399618 | bytes 224601 | solution.py:62
  369.5 35.5 %while.132 = (s32[]{:T(128)}, f32[16,16,8,16]{3,2,0,1:T(8,128)S(1)}, f32[16,16,8]{1,2,0:T(8,128)}, f32[16,8,8]{2,1,0:T(8,128)S(1)}, f32[16,16,8,16]{3,0,2,1:T(8,128)}, /*index=5*/s32[]{:T(128)}) while((s32[]{:T(128)}, f32[16,16,8,16]{3,2,0,1:T(8,128)S(1)}, f32[16,16,8]{1,2,0:T(8,128)}, f32[16,8,8]{2,1,0:T(8,128)S(1)}, ...), condition=%wide.region_3.4_spmd.clone, body=%wide.region_2.3_spmd.clone.sunk | while | flops 199746 | bytes 232601 | solution.py:62
  404.9 2.6 fusion.55
  407.6 35.5 %while.133 = (s32[]{:T(128)}, f32[16,16,8,16]{3,2,0,1:T(8,128)S(1)}, f32[16,16,8]{1,2,0:T(8,128)}, f32[16,8,8]{2,1,0:T(8,128)S(1)}, f32[16,16,8,16]{3,0,2,1:T(8,128)}, /*index=5*/s32[]{:T(128)}) while((s32[]{:T(128)}, f32[16,16,8,16]{3,2,0,1:T(8,128)S(1)}, f32[16,16,8]{1,2,0:T(8,128)}, f32[16,8,8]{2,1,0:T(8,128)S(1)}, ...), condition=%wide.region_8.9_spmd.clone, body=%wide.region_7.8_spmd.clone.sunk | while | flops 199746 | bytes 232601 | solution.py:62
  445.6 3.8 fusion.50
  450.9 10.0 %while.131 = (s32[]{:T(128)}, f32[8,16,16,128]{3,2,1,0:T(8,128)S(1)}, s32[]{:T(128)}, bf16[8,8,16]{2,1,0:T(8,128)(2,1)S(1)}, bf16[8,8,16,16,128]{4,3,2,1,0:T(8,1...) while((s32[]{:T(128)}, f32[8,16,16,128]{3,2,1,0:T(8,128)S(1)}, s32[]{:T(128)}, ...), condition=%wide.region_20.21_spmd, body=%wide.region_19.20_spmd.sunk | while | flops 786566 | bytes 2622875 | solution.py:46
  460.9 3.8 fusion.48
  466.3 2.5 while.128
  468.9 7.4 %fusion.54 = f32[16,8,16,16]{3,1,2,0:T(8,128)S(1)} fusion(f32[16,8,16,16]{3,1,2,0:T(8,128)S(1)} %copy-done.3, f32[16,16,16,128]{3,2,1,0:T(8,128)S(1)} %get-tuple-element.486, f32[16,8,16]{1,2,0:T(8,128)S(1)} %copy-done.4, bf16[16,8,256]{2,1,0:T(8,128)(2,1)S(1)} %copy-done.6), kind=kOutput, calls=%fused_computation.87 | convolution fusion | flops 50397184 | bytes 3440640 | tf_op jit(solution)/shard_map/lks,lhps->lkhp/dot_general | solution.py:159
  477.6 59.3 %all-gather.17.cloned.1.call-done = bf16[256,16,16,128]{3,2,1,0:T(8,128)(2,1)} async-done(((bf16[16,16,16,128]{3,2,1,0:T(8,128)(2,1)}), bf16[256,16,16,128]{3,2,1,0:T(8,128)(2,1)}) %all-gather.17.cloned.1.call-update) | async-done | bytes 16777232 | tf_op jit(solution)/shard_map/all_gather | solution.py:31
  537.1 34.7 %while.129 = (s32[]{:T(128)}, f32[16,16,16,128]{3,2,1,0:T(8,128)S(1)}, s32[]{:T(128)}, bf16[16,16,16]{2,1,0:T(8,128)(2,1)}, bf16[16,16,16,16,128]{4,3,2,1,0:T(8,...) while((s32[]{:T(128)}, f32[16,16,16,128]{3,2,1,0:T(8,128)S(1)}, s32[]{:T(128)}, ...), condition=%wide.region_10.11_spmd, body=%wide.region_9.10_spmd.sunk | while | flops 1573126 | bytes 5245595 | solution.py:46
  571.8 8.2 %fusion.52 = f32[16,8,16,16]{3,1,2,0:T(8,128)S(1)} fusion(f32[16,8,16,16]{3,1,2,0:T(8,128)S(1)} %copy-done.2, f32[16,16,16,128]{3,2,1,0:T(8,128)S(1)} %get-tuple-element.488, f32[16,8,16]{1,2,0:T(8,128)S(1)} %copy.181, bf16[16,8,128]{2,1,0:T(8,128)(2,1)} %copy-done.10), kind=kOutput, calls=%fused_computation.83 | convolution fusion | flops 50397184 | bytes 2400256 | tf_op jit(solution)/shard_map/lks,lhps->lkhp/dot_general | solution.py:159
  (510 shorter events, 191.4 us)
Async XLA Ops:
  6.5 183.3 %copy-start = (bf16[256,512]{1,0:T(8,128)(2,1)S(1)}, bf16[256,512]{1,0:T(8,128)(2,1)}, u32[]{:S(2)}) copy-start(bf16[256,512]{1,0:T(8,128)(2,1)} %param.36) | copy-start | bytes 786436
  6.5 200.7 %copy-start.26 = (bf16[256,64]{0,1:T(8,128)(2,1)S(1)}, bf16[256,64]{0,1:T(8,128)(2,1)}, u32[]{:S(2)}) copy-start(bf16[256,64]{0,1:T(8,128)(2,1)} %param.39) | copy-start | bytes 98308
  6.5 201.0 %copy-start.25 = (f32[16,8]{0,1:T(8,128)S(1)}, f32[16,8]{0,1:T(8,128)}, u32[]{:S(2)}) copy-start(f32[16,8]{0,1:T(8,128)} %param.43) | copy-start | bytes 1540
  6.5 202.0 %copy-start.16 = (bf16[256,1024]{1,0:T(8,128)(2,1)S(1)}, bf16[256,1024]{1,0:T(8,128)(2,1)}, u32[]{:S(2)}) copy-start(bf16[256,1024]{1,0:T(8,128)(2,1)} %param.38) | copy-start | bytes 1572868
  6.5 438.2 %all-gather.19.cloned.1.call-start = ((), (), s32[]{:S(2)}) async-start(), calls=%async_computation.2 | async-start | bytes 4718592 | tf_op jit(solution)/shard_map/all_gather | solution.py:31
  188.9 17.9 %copy-start.23 = (f32[8,256]{1,0:T(8,128)}, f32[8,256]{1,0:T(8,128)S(1)}, u32[]{:S(2)}) copy-start(f32[8,256]{1,0:T(8,128)S(1)} %fusion.94) | copy-start | bytes 24580
  190.9 15.8 %copy-start.20 = (bf16[16,8,512]{2,1,0:T(8,128)(2,1)}, bf16[16,8,512]{2,1,0:T(8,128)(2,1)S(1)}, u32[]{:S(2)}) copy-start(bf16[16,8,512]{2,1,0:T(8,128)(2,1)S(1)} %fusion.60) | copy-start | bytes 393220
  190.9 8.7 %collective-permute-start.1 = (bf16[1,8,256]{2,1,0:T(8,128)(2,1)S(1)}, bf16[1,8,256]{2,1,0:T(8,128)(2,1)S(1)}, u32[]{:S(2)}, u32[]{:S(2)}) collective-permute-start(bf16[1,8,256]{2,1,0:T(8,128)(2,1)S(1)} %get-tuple-element.727), channel_id=1, source_target_pairs={{16,0},{32,16},{48,32},{64,48},{80,64},{96,80},{112,96},{17,1},{33... | collective-permute-start | bytes 12296 | tf_op jit(solution)/shard_map/ppermute | solution.py:19
  192.2 7.4 %collective-permute-start = (bf16[1,8,256]{2,1,0:T(8,128)(2,1)S(1)}, bf16[1,8,256]{2,1,0:T(8,128)(2,1)S(1)}, u32[]{:S(2)}, u32[]{:S(2)}) collective-permute-start(bf16[1,8,256]{2,1,0:T(8,128)(2,1)S(1)} %get-tuple-element.726), channel_id=1, source_target_pairs={{0,16},{16,32},{32,48},{48,64},{64,80},{80,96},{96,112},{1,17},{17... | collective-permute-start | bytes 12296 | tf_op jit(solution)/shard_map/ppermute | solution.py:17
  199.6 5.1 collective-permute-start.2
  201.6 5.1 collective-permute-start.3
  208.7 125.5 %copy-start.14 = (bf16[16,8,128]{2,1,0:T(8,128)(2,1)}, bf16[16,8,128]{2,1,0:T(8,128)(2,1)S(1)}, u32[]{:S(2)}) copy-start(bf16[16,8,128]{2,1,0:T(8,128)(2,1)S(1)} %get-tuple-element.754) | copy-start | bytes 98308
  211.7 239.1 %all-gather.21.cloned.1.call-start = ((), (), s32[]{:S(2)}) async-start(), calls=%async_computation.3 | async-start | bytes 4718592 | tf_op jit(solution)/shard_map/all_gather | solution.py:31
  217.0 249.1 %all-gather.15.cloned.1.call-start = ((), (), s32[]{:S(2)}) async-start(), calls=%async_computation | async-start | bytes 17825792 | tf_op jit(solution)/shard_map/all_gather | solution.py:31
  218.1 105.9 %copy-start.5 = (bf16[16,8,256]{2,1,0:T(8,128)(2,1)}, bf16[16,8,256]{2,1,0:T(8,128)(2,1)S(1)}, u32[]{:S(2)}) copy-start(bf16[16,8,256]{2,1,0:T(8,128)(2,1)S(1)} %fusion.62) | copy-start | bytes 196612
  223.4 313.5 %all-gather.17.cloned.1.call-start = ((), (), s32[]{:S(2)}) async-start(), calls=%async_computation.1 | async-start | bytes 17825792 | tf_op jit(solution)/shard_map/all_gather | solution.py:31
  223.8 110.5 %copy-start.8 = (f32[8,16,16]{1,2,0:T(8,128)}, f32[8,16,16]{1,2,0:T(8,128)S(1)}, u32[]{:S(2)}) copy-start(f32[8,16,16]{1,2,0:T(8,128)S(1)} %copy.193) | copy-start | bytes 24580
  224.5 103.4 %copy-start.12 = (bf16[8,16,128]{2,1,0:T(8,128)(2,1)}, bf16[8,16,128]{2,1,0:T(8,128)(2,1)S(1)}, u32[]{:S(2)}) copy-start(bf16[8,16,128]{2,1,0:T(8,128)(2,1)S(1)} %rev.51) | copy-start | bytes 98308
  227.7 100.3 %copy-start.10 = (bf16[16,8,128]{2,1,0:T(8,128)(2,1)}, bf16[16,8,128]{2,1,0:T(8,128)(2,1)S(1)}, u32[]{:S(2)}) copy-start(bf16[16,8,128]{2,1,0:T(8,128)(2,1)S(1)} %rev.45) | copy-start | bytes 98308
  404.9 38.2 %copy-start.11 = (bf16[16,8,128]{2,1,0:T(8,128)(2,1)S(1)}, bf16[16,8,128]{2,1,0:T(8,128)(2,1)}, u32[]{:S(2)}) copy-start(bf16[16,8,128]{2,1,0:T(8,128)(2,1)} %copy-done.10) | copy-start | bytes 98308
  450.9 10.0 %copy-start.7 = (f32[8,16,16]{1,2,0:T(8,128)S(1)}, f32[8,16,16]{1,2,0:T(8,128)}, u32[]{:S(2)}) copy-start(f32[8,16,16]{1,2,0:T(8,128)} %copy.205) | copy-start | bytes 24580
  450.9 10.0 %copy-start.13 = (bf16[8,16,128]{2,1,0:T(8,128)(2,1)S(1)}, bf16[8,16,128]{2,1,0:T(8,128)(2,1)}, u32[]{:S(2)}) copy-start(bf16[8,16,128]{2,1,0:T(8,128)(2,1)} %copy-done.12) | copy-start | bytes 98308
  537.1 34.7 %copy-start.2 = (f32[16,8,16,16]{3,1,2,0:T(8,128)S(1)}, f32[16,8,16,16]{3,1,2,0:T(8,128)}, u32[]{:S(2)}) copy-start(f32[16,8,16,16]{3,1,2,0:T(8,128)} %fusion.53) | copy-start | bytes 393220
  571.8 10.3 %copy-start.1 = (bf16[256,512]{1,0:T(8,128)(2,1)S(1)}, bf16[256,512]{1,0:T(8,128)(2,1)}, u32[]{:S(2)}) copy-start(bf16[256,512]{1,0:T(8,128)(2,1)} %param.36) | copy-start | bytes 786436
  (13 other events, 18.0 us)
Sparse Core Ops, SparseCore 0:
  211.9 66.4 all-gather.18
  280.7 69.7 all-gather.20
  352.2 90.3 all-gather.14
  444.2 92.6 all-gather.16
where the time goes:
time: 596 us; the launch traced here: 589 us
  blocking collectives  277 us (46%)
  local copies, waits for them, and re-layouts  102 us (17%)
  matrix products  64 us (11%)
  waiting for transfers between devices  61.3 us (10%)
  other arithmetic  56 us (9%)
  between operations  14.1 us (2%)
  starting transfers between devices  11.3 us (2%)
    all_gather x1, blocking collectives, per_device(): lax.all_gather(local_tokens, ('row', 'col'), axis=0, tiled=True)  180 us
    all_gather x4, blocking collectives, entering(): lax.all_gather(a.astype(kind), axis)  96.2 us
    all_gather x4, waiting for transfers between devices, entering(): lax.all_gather(a.astype(kind), axis)  59.3 us
    dynamic_slice x64, local copies, waits for them, and re-layouts, segment_recurrence(): lax.map(head_term, (jnp.moveaxis(cumulative, 2, 0), jnp.moveaxis(driven,...  53.9 us
    add x22, other arithmetic, combine_states(): later[0][:, :, None, None] * earlier[1] + later[1]  35.5 us
    sub x96, local copies, waits for them, and re-layouts, head_term(): head_cum[:, :, None] - head_cum[:, None, :]  35.3 us
    dot_general x4, matrix products, finish(): jnp.einsum('lks,lhps->lkhp', out_l.astype(jnp.float32), inflow, precision...  23.2 us
    dot_general x64, matrix products, head_term(): jnp.einsum('lkj,ljp->lkp', scores * jnp.exp(spread), head_drive, precisio...  18.7 us
  transfers between devices with their start and end apart: 8, of which 2 were waited for; matrix products, arithmetic and copies ran while one was open for 29% of the time, Pallas kernels for 0%

commit v1 on v0

v1 whole, which is shorter than its diff:
```python
import jax
import jax.numpy as jnp
from jax import lax
from jax.experimental import pallas as pl
from jax.experimental.pallas import tpu as pltpu
from jax.sharding import PartitionSpec as P

F32 = jnp.float32
BF16 = jnp.bfloat16
ROWS = 8
COLS = 16
TR = 16
TC = 8
LINE = 128
D = 256
HEADS = 16
HEAD_DIM = 16
STATE = 128
precise = lax.Precision.HIGHEST


def iota(shape, dim):
    return lax.broadcasted_iota(jnp.int32, shape, dim)


def halves(x):
    high = x.astype(BF16).astype(F32)
    return high, x - high


def silu(x):
    return x * jax.nn.sigmoid(x)


def pack_row_kernel(latent_ref, logs_ref, horizon_ref, out_ref):
    r = lax.axis_index("row")
    target = iota((LINE, LINE), 0)
    source = iota((LINE, LINE), 1)
    pick = ((target % TR) * TC + target // TR == source).astype(BF16)
    flat = latent_ref[...].astype(F32).reshape(LINE, D).astype(BF16)
    columns = jnp.dot(pick, flat, preferred_element_type=F32).astype(BF16)
    halo = jnp.concatenate(
        [latent_ref[0].astype(F32), latent_ref[TR - 1].astype(F32)], axis=0
    ).astype(BF16)
    row8 = iota((8, D), 0)
    logs = jnp.where(row8 == r, jnp.broadcast_to(logs_ref[...].astype(F32), (8, D)), 0.0)
    here = iota((TR, LINE), 1) - TR * r == iota((TR, LINE), 0)
    for dest in range(ROWS):
        for slot in range(3):
            j = (dest + slot - 1) % ROWS
            out_ref[dest, slot * TR : (slot + 1) * TR, :] = columns[j * TR : (j + 1) * TR, :]
        out_ref[dest, 48:64, :] = halo
        column = jnp.broadcast_to(horizon_ref[:, dest : dest + 1], (TR, LINE))
        line = jnp.sum(jnp.where(here, column, 0.0), axis=0, keepdims=True)
        high, low = halves(line)
        meta = jnp.concatenate([high, low], axis=1)
        meta = jnp.where(row8 == 0, jnp.broadcast_to(meta, (8, D)), 0.0)
        out_ref[dest, 64:80, :] = jnp.concatenate([logs, meta], axis=0).astype(BF16)


def pack_col_kernel(trace_ref, got_ref, latent_ref, horizon_ref, out_ref, side_ref):
    r = lax.axis_index("row")
    c = lax.axis_index("col")
    above = got_ref[jnp.maximum(r - 1, 0), 48:64, :].astype(F32)[8:16]
    below = got_ref[jnp.minimum(r + 1, ROWS - 1), 48:64, :].astype(F32)[0:8]
    own = latent_ref[...].astype(F32)
    logs = jnp.sum(got_ref[:, 64:80, :].astype(F32)[:, 0:8, :], axis=0)
    lane = iota((TR, LINE), 1) - TC * c
    spread = jnp.zeros((TR, LINE), F32)
    lane1 = iota((1, LINE), 1) - TC * c
    trace = jnp.zeros((1, LINE), F32)
    for j in range(TC):
        column = jnp.broadcast_to(horizon_ref[:, j : j + 1], (TR, LINE))
        spread = jnp.where(lane == j, column, spread)
        trace = jnp.where(lane1 == j, trace_ref[j].astype(F32), trace)
    high, low = halves(spread)
    first = jnp.concatenate([jnp.broadcast_to(trace, (TR, LINE)), high], axis=1)
    second = jnp.concatenate([low, jnp.zeros((TR, LINE), F32)], axis=1)
    row16 = iota((16, D), 0)
    rows = [above] + [own[i] for i in range(TR)] + [below]
    for dest in range(COLS):
        pair = jnp.concatenate([rows[dest], rows[dest + 1]], axis=0)
        out_ref[dest, 0:16, :] = pair.astype(BF16)
        pair = jnp.concatenate([rows[dest + 2], logs], axis=0)
        out_ref[dest, 16:32, :] = pair.astype(BF16)
        meta = jnp.where(row16 == 0, jnp.broadcast_to(first[dest : dest + 1], (16, D)), 0.0)
        meta = jnp.where(row16 == 1, jnp.broadcast_to(second[dest : dest + 1], (16, D)), meta)
        out_ref[dest, 32:48, :] = meta.astype(BF16)
    left = got_ref[:, 0:16, :]
    right = got_ref[:, 32:48, :]
    side_ref[...] = jnp.where(r == 0, left, right)


def normalised(hidden, gain):
    scale = lax.rsqrt(jnp.mean(hidden * hidden, axis=-1, keepdims=True) + 1e-06)
    return (hidden * scale * gain).astype(BF16)


def line_scan(cells, tokens, inside, taps, gain, in_w, bc, dt_w, bias, rate, horizon, w_ref, x_ref):
    pre = []
    for s in range(3):
        n = normalised(cells[s] + tokens[s], gain)
        p = jnp.dot(n, in_w, preferred_element_type=F32).astype(BF16).astype(F32)
        pre.append(jnp.where(inside[s], p, 0.0))
    shifted = [
        taps[t][0] * pre[0] + taps[t][1] * pre[1] + taps[t][2] * pre[2] for t in range(3)
    ]
    place = iota((LINE, D), 0)
    conv = (
        shifted[1]
        + jnp.where(place == 0, 0.0, pltpu.roll(shifted[0], 1, 0))
        + jnp.where(place == LINE - 1, 0.0, pltpu.roll(shifted[2], LINE - 1, 0))
    )
    mixed = silu(conv).astype(BF16)
    coef = jnp.dot(mixed, bc, preferred_element_type=F32).astype(BF16)
    contract = (((1,), (1,)), ((), ()))
    k = iota((LINE, LINE), 0)
    j = iota((LINE, LINE), 1)
    lower = j <= k
    score_f = lax.dot_general(
        coef[:, STATE : 2 * STATE], coef[:, :STATE], contract, preferred_element_type=F32
    )
    score_b = lax.dot_general(
        coef[:, 3 * STATE :], coef[:, 2 * STATE : 3 * STATE], contract, preferred_element_type=F32
    )
    score_f = jnp.where(lower, score_f, 0.0)
    score_b = jnp.where(j >= k, score_b, 0.0)
    steps = []
    sums_t = []
    sums = []
    for side in range(2):
        z = jnp.dot(mixed, dt_w[side], preferred_element_type=F32) + bias[side]
        step = jnp.maximum(z, 0.0) + jnp.log1p(jnp.exp(-jnp.abs(z)))
        decay_t = (-step * rate[side]).T - horizon
        ones = (k <= j) if side == 0 else (k >= j)
        total = jnp.dot(decay_t, ones.astype(F32), precision=precise, preferred_element_type=F32)
        steps.append(step.T)
        sums_t.append(total)
        sums.append(total.T)
    head_of = iota((LINE, D), 1) // HEAD_DIM
    wide = mixed.astype(F32)
    for h in range(HEADS):
        ahead = sums[0][:, h : h + 1] - sums_t[0][h : h + 1, :]
        behind = sums[1][:, h : h + 1] - sums_t[1][h : h + 1, :]
        decay = jnp.exp(jnp.where(lower, ahead, behind))
        drive = score_f * steps[0][h : h + 1, :] + score_b * steps[1][h : h + 1, :]
        w_ref[:, h * LINE : (h + 1) * LINE] = (drive * decay).astype(BF16)
        x_ref[h * LINE : (h + 1) * LINE, :] = jnp.where(head_of == h, wide, 0.0).astype(BF16)
    return jnp.dot(w_ref[...], x_ref[...], preferred_element_type=F32)


def column_kernel(
    rows_ref,
    side_ref,
    cols_ref,
    cond_ref,
    gain_ref,
    in_ref,
    conv_ref,
    bc_ref,
    dt_ref,
    bias_ref,
    rate_ref,
    out_ref,
    tokens_ref,
    w_ref,
    x_ref,
):
    r = lax.axis_index("row")
    c = lax.axis_index("col")
    logs = cols_ref[:, 16:32, :].astype(F32)[:, 8:16, :].reshape(LINE, D).astype(BF16)
    tokens = silu(jnp.dot(logs, cond_ref[...], preferred_element_type=F32)).astype(BF16)
    meta = jnp.sum(cols_ref[:, 32:48, :].astype(F32), axis=0)
    trace = meta[0:1, 0:LINE].astype(jnp.int32)
    position = iota((LINE, LINE), 0)
    names = (position % ROWS) * COLS + position // ROWS
    chosen = (names == trace).astype(F32).T.astype(BF16)
    tokens_ref[...] = jnp.dot(chosen, tokens, preferred_element_type=F32)
    column = c * TC + r
    cells = [
        rows_ref[:, s * TR : (s + 1) * TR, :].astype(F32).reshape(LINE, D) for s in range(3)
    ]
    side = side_ref[...].astype(F32).reshape(LINE, D)
    cells[0] = jnp.where(r == 0, side, cells[0])
    cells[2] = jnp.where(r == ROWS - 1, side, cells[2])
    lines = [jnp.maximum(column - 1, 0), column, jnp.minimum(column + 1, LINE - 1)]
    line_tokens = [tokens_ref[pl.ds(x, 1), :] for x in lines]
    hor = jnp.sum(rows_ref[:, 64:80, :].astype(F32), axis=0)[8:9]
    horizon = hor[:, :LINE] + hor[:, LINE:]
    out_ref[...] = line_scan(
        cells,
        line_tokens,
        [column > 0, True, column < LINE - 1],
        [[conv_ref[3 * t + s : 3 * t + s + 1, :] for s in range(3)] for t in range(3)],
        gain_ref[...],
        in_ref[:, :D],
        bc_ref[:, 4 * STATE :],
        [dt_ref[:, 2 * HEADS : 3 * HEADS], dt_ref[:, 3 * HEADS :]],
        [bias_ref[2:3, :], bias_ref[3:4, :]],
        [rate_ref[0:1, :] / 2048.0, rate_ref[1:2, :] / 2048.0],
        horizon,
        w_ref,
        x_ref,
    ).astype(BF16)


def row_kernel(
    cols_ref,
    tokens_ref,
    gain_ref,
    in_ref,
    conv_ref,
    bc_ref,
    dt_ref,
    bias_ref,
    rate_ref,
    out_ref,
    w_ref,
    x_ref,
):
    r = lax.axis_index("row")
    c = lax.axis_index("col")
    row = r * TR + c
    pair = cols_ref[:, 0:16, :].astype(F32)
    last = cols_ref[:, 16:32, :].astype(F32)
    cells = [pair[:, 0:8, :], pair[:, 8:16, :], last[:, 0:8, :]]
    cells = [x.reshape(LINE, D) for x in cells]
    tokens = tokens_ref[...]
    meta = jnp.sum(cols_ref[:, 32:48, :].astype(F32), axis=0)
    horizon = meta[0:1, LINE:] + meta[1:2, :LINE]
    out_ref[...] = line_scan(
        cells,
        [tokens, tokens, tokens],
        [row > 0, True, row < LINE - 1],
        [[conv_ref[3 * s + t : 3 * s + t + 1, :] for s in range(3)] for t in range(3)],
        gain_ref[...],
        in_ref[:, :D],
        bc_ref[:, : 4 * STATE],
        [dt_ref[:, :HEADS], dt_ref[:, HEADS : 2 * HEADS]],
        [bias_ref[0:1, :], bias_ref[1:2, :]],
        [rate_ref[0:1, :] / 2048.0, rate_ref[1:2, :] / 2048.0],
        horizon,
        w_ref,
        x_ref,
    ).astype(BF16)


def tile_kernel(latent_ref, tokens_ref, gain_ref, in_ref, hidden_ref, gate_ref):
    c = lax.axis_index("col")
    own = tokens_ref[pl.ds(c * TC, TC), :]
    hidden = (latent_ref[...].astype(F32) + own[None]).reshape(LINE, D)
    hidden_ref[...] = hidden
    n = normalised(hidden, gain_ref[...])
    gate = jnp.dot(n, in_ref[:, D:], preferred_element_type=F32).astype(BF16).astype(F32)
    gate_ref[...] = silu(gate)


def finish_kernel(row_ref, col_ref, hidden_ref, gate_ref, gain_ref, out_w_ref, out_ref):
    target = iota((LINE, LINE), 0)
    source = iota((LINE, LINE), 1)
    pick = ((target % TC) * TR + target // TC == source).astype(BF16)
    by_column = jnp.dot(pick, col_ref[...].reshape(LINE, D), preferred_element_type=F32)
    total = row_ref[...].astype(F32).reshape(LINE, D) + by_column
    scale = lax.rsqrt(jnp.mean(total * total, axis=-1, keepdims=True) + 1e-05)
    gated = (total * scale * gain_ref[...] * gate_ref[...]).astype(BF16)
    branch = jnp.dot(gated, out_w_ref[...], preferred_element_type=F32)
    out_ref[...] = (hidden_ref[...] + branch).reshape(TR, TC, D).astype(BF16)


def call(kernel, outs, *args, scratch=(), smem_first=False):
    vmem = pl.BlockSpec(memory_space=pltpu.VMEM)
    specs = [vmem] * len(args)
    if smem_first:
        specs[0] = pl.BlockSpec(memory_space=pltpu.SMEM)
    return pl.pallas_call(
        kernel,
        out_shape=[jax.ShapeDtypeStruct(s, d) for s, d in outs],
        in_specs=specs,
        out_specs=[vmem] * len(outs),
        scratch_shapes=list(scratch),
        name=kernel.__name__,
    )(*args)


def per_device(
    latent,
    well_logs,
    cond_weight,
    trace_rows,
    norm_gain,
    in_weight,
    conv_weight,
    bc_weight,
    dt_weight,
    dt_bias,
    row_rate,
    col_rate,
    horizon,
    out_gain,
    out_weight,
):
    gain = norm_gain.reshape(1, D)
    final_gain = out_gain.reshape(1, D)
    (packed,) = call(
        pack_row_kernel, [((ROWS, 80, D), BF16)], latent, well_logs, horizon
    )
    from_rows = lax.all_to_all(packed, "row", 0, 0, tiled=True)
    packed, side = call(
        pack_col_kernel,
        [((COLS, 48, D), BF16), ((ROWS, TR, D), BF16)],
        trace_rows,
        from_rows,
        latent,
        horizon,
        smem_first=True,
    )
    neighbours = [(i, i + 1) for i in range(COLS - 1)]
    last = (ROWS - 1) * COLS
    neighbours += [(last + i + 1, last + i) for i in range(COLS - 1)]
    side = lax.ppermute(side, ("row", "col"), neighbours)
    from_cols = lax.all_to_all(packed, "col", 0, 0, tiled=True)
    scratch = [pltpu.VMEM((LINE, HEADS * LINE), BF16), pltpu.VMEM((HEADS * LINE, D), BF16)]
    by_column, tokens = call(
        column_kernel,
        [((LINE, D), BF16), ((LINE, D), F32)],
        from_rows,
        side,
        from_cols,
        cond_weight,
        gain,
        in_weight,
        conv_weight,
        bc_weight,
        dt_weight,
        dt_bias,
        col_rate,
        scratch=scratch,
    )
    by_column = lax.all_to_all(by_column.reshape(ROWS, TR, D), "row", 0, 0, tiled=True)
    (by_row,) = call(
        row_kernel,
        [((LINE, D), BF16)],
        from_cols,
        tokens,
        gain,
        in_weight,
        conv_weight,
        bc_weight,
        dt_weight,
        dt_bias,
        row_rate,
        scratch=scratch,
    )
    by_row = lax.all_to_all(by_row.reshape(COLS, TC, D), "col", 0, 0, tiled=True)
    hidden, gate = call(
        tile_kernel, [((LINE, D), F32), ((LINE, D), F32)], latent, tokens, gain, in_weight
    )
    (out,) = call(
        finish_kernel,
        [((TR, TC, D), BF16)],
        by_row,
        by_column,
        hidden,
        gate,
        final_gain,
        out_weight,
    )
    return out


def solution(mesh):
    placed = (
        P("row", "col", None),
        P(("row", "col"), None),
        P(),
        P("col"),
        P(),
        P(),
        P(),
        P(),
        P(),
        P(),
        P(),
        P(),
        P("row", "col"),
        P(),
        P(),
    )
    return jax.shard_map(
        per_device, mesh=mesh, in_specs=placed, out_specs=P("row", "col", None), check_vma=False
    )
```

time: 596 us -> 67.7 us (0.11); the launches traced: 589 us -> 67 us
  blocking collectives: 277 us -> 15.9 us
  local copies, waits for them, and re-layouts: 102 us -> 4.06 us
  matrix products: 64 us -> 0 us
  other arithmetic: 56 us -> 0 us
  waiting for transfers between devices: 61.3 us -> 10.5 us
  Pallas kernels: 0 us -> 16.2 us
  between operations: 14.1 us -> 0.04 us
  starting transfers between devices: 11.3 us -> 20.2 us
    all_gather x5 -> x0, blocking collectives: 277 us -> none  [the longest x1 180 us: per_device(): lax.all_gather(local_tokens, ('row', 'col'), axis=0, tiled=True)]
    dot_general x92 -> x0, matrix products: 64 us -> none  [the longest x4 23.2 us: finish(): jnp.einsum('lks,lhps->lkhp', out_l.astype(jnp.float32), inflow, precision...]
    all_gather x4 -> x0, waiting for transfers between devices: 59.3 us -> none  [entering(): lax.all_gather(a.astype(kind), axis)]
    dynamic_slice x64 -> x0, local copies, waits for them, and re-layouts: 53.9 us -> none  [segment_recurrence(): lax.map(head_term, (jnp.moveaxis(cumulative, 2, 0), jnp.moveaxis(driven,...]
    add x22 -> x0, other arithmetic: 35.5 us -> none  [combine_states(): later[0][:, :, None, None] * earlier[1] + later[1]]
    sub x97 -> x0, local copies, waits for them, and re-layouts: 35.4 us -> none  [the longest x96 35.3 us: head_term(): head_cum[:, :, None] - head_cum[:, None, :]]
    all_to_all x0 -> x3, starting transfers between devices: none -> 16.7 us  [the longest x1 7.71 us: per_device(): from_cols = lax.all_to_all(packed, 'col', 0, 0, tiled=True)]
    pallas_call x0 -> x6, Pallas kernels: none -> 16.2 us  [call(): pl.pallas_call(kernel, out_shape=[jax.ShapeDtypeStruct(s, d) for s, d in...]
  transfers between devices with their start and end apart: 8 -> 4, of which waited for: 2 -> 4; matrix products, arithmetic and copies ran while one was open for 29% -> 1% of each run, Pallas kernels for 0% -> 9%
where the time goes in v1:
time: 67.7 us; the launch traced here: 67 us
  starting transfers between devices  20.2 us (30%)
  Pallas kernels  16.2 us (24%)
  blocking collectives  15.9 us (23%)
  waiting for transfers between devices  10.5 us (16%)
  local copies, waits for them, and re-layouts  4.06 us (6%)
    pallas_call x6, Pallas kernels, call(): pl.pallas_call(kernel, out_shape=[jax.ShapeDtypeStruct(s, d) for s, d in...  16.2 us
    all_to_all x1, blocking collectives, per_device(): from_rows = lax.all_to_all(packed, 'row', 0, 0, tiled=True)  15.9 us
    all_to_all x1, starting transfers between devices, per_device(): from_cols = lax.all_to_all(packed, 'col', 0, 0, tiled=True)  7.71 us
    all_to_all x1, starting transfers between devices, per_device(): lax.all_to_all(by_row.reshape(COLS, TC, D), 'col', 0, 0, tiled=True)  5.64 us
    unnamed x14, local copies, waits for them, and re-layouts  4.06 us
    all_to_all x1, waiting for transfers between devices, per_device(): lax.all_to_all(by_row.reshape(COLS, TC, D), 'col', 0, 0, tiled=True)  3.9 us
    ppermute x1, starting transfers between devices, per_device(): side = lax.ppermute(side, ('row', 'col'), neighbours)  3.54 us
    all_to_all x1, starting transfers between devices, per_device(): lax.all_to_all(by_column.reshape(ROWS, TR, D), 'row', 0, 0, tiled=True)  3.35 us
  transfers between devices with their start and end apart: 4, of which 4 were waited for; matrix products, arithmetic and copies ran while one was open for 1% of the time, Pallas kernels for 9%

profile of v1, /device:TPU:1, one launch (start us, length us, event | category | flops | bytes accessed | tf_op | source)
XLA Modules:
  0.0 67.0 jit_solution(4406083423296697625)
XLA Ops:
  0.0 1.3 %copy.16.horizon_ref = f32[16,8]{1,0:T(8,128)} copy(f32[16,8]{0,1:T(8,128)} %param.27) | data formatting | bytes 1024 | tf_op args[12]
  1.3 1.7 %pack_row_kernel.1 = bf16[8,80,256]{2,1,0:T(8,128)(2,1)} custom-call(bf16[16,8,256]{2,1,0:T(8,128)(2,1)} %latent_ref.5, bf16[1,256]{1,0:T(2,128)(2,1)} %logs_ref.1, f32[16,8]{1,0:T(8,128)} %copy.16.horizon_ref), custom_call_target="tpu_custom_call" | custom-call | tf_op jit(solution)/shard_map/pack_row_kernel/pallas_call | solution.py:275
  3.1 15.9 %all_to_all.20.got_ref.rows_ref = bf16[8,80,256]{2,1,0:T(8,128)(2,1)} all-to-all(bf16[8,80,256]{2,1,0:T(8,128)(2,1)} %pack_row_kernel.1), channel_id=1, replica_groups=mesh['row'=8,'col'=16] {'row'}, dimensions={0} | all-to-all | bytes 655360 | tf_op jit(solution)/shard_map/all_to_all | solution.py:307
  19.0 1.9 %pack_col_kernel.1 = (bf16[16,48,256]{2,1,0:T(8,128)(2,1)}, bf16[8,16,256]{2,1,0:T(8,128)(2,1)}) custom-call(s32[8]{0:T(128)} %trace_ref.1, bf16[8,80,256]{2,1,0:T(8,128)(2,1)} %all_to_all.20.got_ref.rows_ref, bf16[16,8,256]{2,1,0:T(8,128)(2,1)} %latent_ref.5, f32[16,8]{1,0:T(8,128)} %copy.16.horizon_ref), custom_call_target="tpu_custom_call" | custom-call | tf_op jit(solution)/shard_map/pack_col_kernel/pallas_call | solution.py:275
  20.9 0.0 copy-start.5
  20.9 7.7 %all-to-all-start.1 = ((bf16[16,48,256]{2,1,0:T(8,128)(2,1)}), bf16[16,48,256]{2,1,0:T(8,128)(2,1)S(1)}, u32[]{:S(2)}, u32[]{:S(2)}) async-start(bf16[16,48,256]{2,1,0:T(8,128)(2,1)} %get-tuple-element.11), calls=%async_computation.1 | async-start | bytes 786432 | tf_op jit(solution)/shard_map/all_to_all | solution.py:321
  28.6 0.0 copy-done.5
  28.6 3.5 %collective-permute-start = (bf16[8,16,256]{2,1,0:T(8,128)(2,1)S(1)}, bf16[8,16,256]{2,1,0:T(8,128)(2,1)S(1)}, u32[]{:S(2)}, u32[]{:S(2)}) collective-permute-start(bf16[8,16,256]{2,1,0:T(8,128)(2,1)S(1)} %copy-done.5), channel_id=1, source_target_pairs={{0,1},{1,2},{2,3},{3,4},{4,5},{5,6},{6,7},{7,8},{8,9},{9,10},{10,1... | collective-permute-start | bytes 196616 | tf_op jit(solution)/shard_map/ppermute | solution.py:320
  32.1 0.0 copy-done.4
  32.1 0.7 %copy.18.dt_ref = bf16[256,64]{1,0:T(8,128)(2,1)} copy(bf16[256,64]{0,1:T(8,128)(2,1)S(1)} %copy-done.4) | data formatting | bytes 65536 | tf_op args[8]
  32.9 1.3 %collective-permute-done.side_ref = bf16[8,16,256]{2,1,0:T(8,128)(2,1)S(1)} collective-permute-done((bf16[8,16,256]{2,1,0:T(8,128)(2,1)S(1)}, bf16[8,16,256]{2,1,0:T(8,128)(2,1)S(1)}, u32[]{:S(2)}, u32[]{:S(2)}) %collective-permute-start) | collective-permute-done | bytes 65568 | tf_op jit(solution)/shard_map/ppermute | solution.py:320
  34.2 2.8 %all-to-all-done.1.cols_ref = bf16[16,48,256]{2,1,0:T(8,128)(2,1)S(1)} async-done(((bf16[16,48,256]{2,1,0:T(8,128)(2,1)}), bf16[16,48,256]{2,1,0:T(8,128)(2,1)S(1)}, u32[]{:S(2)}, u32[]{:S(2)}) %all-to-all-start.1) | async-done | bytes 393248 | tf_op jit(solution)/shard_map/all_to_all | solution.py:321
  37.0 0.0 copy-done.3
  37.0 0.7 %copy-done = bf16[16,48,256]{2,1,0:T(8,128)(2,1)} copy-done((bf16[16,48,256]{2,1,0:T(8,128)(2,1)}, bf16[16,48,256]{2,1,0:T(8,128)(2,1)S(1)}, u32[]{:S(2)}) %copy-start) | copy-done | bytes 393240
  37.7 4.5 %column_kernel.1 = (bf16[128,256]{1,0:T(8,128)(2,1)}, f32[128,256]{1,0:T(8,128)}) custom-call(bf16[8,80,256]{2,1,0:T(8,128)(2,1)} %all_to_all.20.got_ref.rows_ref, bf16[8,16,256]{2,1,0:T(8,128)(2,1)} %copy-done.3, bf16[16,48,256]{2,1,0:T(8,128)(2,1)} %copy-done, bf16[256,256]{1,0:T(8,128)(2,1)} %cond_ref.1, f32[1,256]{1,0:T(1,128)} %bitcast.6, ...), custom_call_target="tpu_custom_call" | custom-call | tf_op jit(solution)/shard_map/column_kernel/pallas_call | solution.py:275
  42.2 3.3 %all-to-all-start.3 = ((bf16[8,16,256]{2,1,0:T(8,128)(2,1)}), bf16[8,16,256]{2,1,0:T(8,128)(2,1)S(1)}, u32[]{:S(2)}, u32[]{:S(2)}) async-start(bf16[8,16,256]{2,1,0:T(8,128)(2,1)} %bitcast.5), calls=%async_computation.3 | async-start | bytes 131072 | tf_op jit(solution)/shard_map/all_to_all | solution.py:339
  45.6 4.0 %row_kernel.1 = bf16[128,256]{1,0:T(8,128)(2,1)} custom-call(bf16[16,48,256]{2,1,0:T(8,128)(2,1)} %copy-done, f32[128,256]{1,0:T(8,128)} %get-tuple-element.13.tokens_ref, f32[1,256]{1,0:T(1,128)} %bitcast.7, bf16[256,512]{1,0:T(8,128)(2,1)} %in_ref.5, f32[9,256]{1,0:T(8,128)} %conv_ref.3, bf16[256,1024]{1,0:T(8,128)(2,1)} %bc_ref.3, ...), custom_call_target="tpu_custom_call" | custom-call | tf_op jit(solution)/shard_map/row_kernel/pallas_call | solution.py:275
  49.6 2.5 %all-to-all-done.3.col_ref = bf16[8,16,256]{2,1,0:T(8,128)(2,1)S(1)} async-done(((bf16[8,16,256]{2,1,0:T(8,128)(2,1)}), bf16[8,16,256]{2,1,0:T(8,128)(2,1)S(1)}, u32[]{:S(2)}, u32[]{:S(2)}) %all-to-all-start.3) | async-done | bytes 65568 | tf_op jit(solution)/shard_map/all_to_all | solution.py:339
  52.1 0.6 copy-done.1
  52.7 5.6 %all-to-all-start.2 = ((bf16[16,8,256]{2,1,0:T(8,128)(2,1)}), bf16[16,8,256]{2,1,0:T(8,128)(2,1)S(1)}, u32[]{:S(2)}, u32[]{:S(2)}) async-start(bf16[16,8,256]{2,1,0:T(8,128)(2,1)} %bitcast.4), calls=%async_computation.2 | async-start | bytes 131072 | tf_op jit(solution)/shard_map/all_to_all | solution.py:354
  58.4 2.0 %tile_kernel.1 = (f32[128,256]{1,0:T(8,128)}, f32[128,256]{1,0:T(8,128)}) custom-call(bf16[16,8,256]{2,1,0:T(8,128)(2,1)} %latent_ref.5, f32[128,256]{1,0:T(8,128)} %get-tuple-element.13.tokens_ref, f32[1,256]{1,0:T(1,128)} %bitcast.8, bf16[256,512]{1,0:T(8,128)(2,1)} %in_ref.5), custom_call_target="tpu_custom_call" | custom-call | tf_op jit(solution)/shard_map/tile_kernel/pallas_call | solution.py:275
  60.3 3.9 %all-to-all-done.2.row_ref = bf16[16,8,256]{2,1,0:T(8,128)(2,1)S(1)} async-done(((bf16[16,8,256]{2,1,0:T(8,128)(2,1)}), bf16[16,8,256]{2,1,0:T(8,128)(2,1)S(1)}, u32[]{:S(2)}, u32[]{:S(2)}) %all-to-all-start.2) | async-done | bytes 65568 | tf_op jit(solution)/shard_map/all_to_all | solution.py:354
  64.3 0.6 copy-done.2
  64.9 2.1 %finish_kernel.1 = bf16[16,8,256]{2,1,0:T(8,128)(2,1)} custom-call(bf16[16,8,256]{2,1,0:T(8,128)(2,1)} %copy-done.2, bf16[8,16,256]{2,1,0:T(8,128)(2,1)} %copy-done.1, f32[128,256]{1,0:T(8,128)} %get-tuple-element.15.hidden_ref, f32[128,256]{1,0:T(8,128)} %get-tuple-element.16.gate_ref, f32[1,256]{1,0:T(1,128)} %bitcast.9, bf16[256,256]{1,0:T(8,128)(2,1)} %out_w_ref.1), custom_call_target="tpu_custom_call" | custom-call | tf_op jit(solution)/shard_map/finish_kernel/pallas_call | solution.py:275
  (5 shorter events, 0.0 us)
Async XLA Ops:
  20.9 7.7 %copy-start.5 = (bf16[8,16,256]{2,1,0:T(8,128)(2,1)S(1)}, bf16[8,16,256]{2,1,0:T(8,128)(2,1)}, u32[]{:S(2)}) copy-start(bf16[8,16,256]{2,1,0:T(8,128)(2,1)} %get-tuple-element.12) | copy-start | bytes 196612
  20.9 11.3 %copy-start.4 = (bf16[256,64]{0,1:T(8,128)(2,1)S(1)}, bf16[256,64]{0,1:T(8,128)(2,1)}, u32[]{:S(2)}) copy-start(bf16[256,64]{0,1:T(8,128)(2,1)} %param.23) | copy-start | bytes 98308
  20.9 16.1 %all-to-all-start.1 = ((bf16[16,48,256]{2,1,0:T(8,128)(2,1)}), bf16[16,48,256]{2,1,0:T(8,128)(2,1)S(1)}, u32[]{:S(2)}, u32[]{:S(2)}) async-start(bf16[16,48,256]{2,1,0:T(8,128)(2,1)} %get-tuple-element.11), calls=%async_computation.1 | async-start | bytes 786432 | tf_op jit(solution)/shard_map/all_to_all | solution.py:321
  28.6 5.6 %collective-permute-start = (bf16[8,16,256]{2,1,0:T(8,128)(2,1)S(1)}, bf16[8,16,256]{2,1,0:T(8,128)(2,1)S(1)}, u32[]{:S(2)}, u32[]{:S(2)}) collective-permute-start(bf16[8,16,256]{2,1,0:T(8,128)(2,1)S(1)} %copy-done.5), channel_id=1, source_target_pairs={{0,1},{1,2},{2,3},{3,4},{4,5},{5,6},{6,7},{7,8},{8,9},{9,10},{10,1... | collective-permute-start | bytes 196616 | tf_op jit(solution)/shard_map/ppermute | solution.py:320
  34.2 2.8 %copy-start.3 = (bf16[8,16,256]{2,1,0:T(8,128)(2,1)}, bf16[8,16,256]{2,1,0:T(8,128)(2,1)S(1)}, u32[]{:S(2)}) copy-start(bf16[8,16,256]{2,1,0:T(8,128)(2,1)S(1)} %collective-permute-done.side_ref) | copy-start | bytes 196612
  37.0 0.7 %copy-start = (bf16[16,48,256]{2,1,0:T(8,128)(2,1)}, bf16[16,48,256]{2,1,0:T(8,128)(2,1)S(1)}, u32[]{:S(2)}) copy-start(bf16[16,48,256]{2,1,0:T(8,128)(2,1)S(1)} %all-to-all-done.1.cols_ref) | copy-start | bytes 1179652
  42.2 9.9 %all-to-all-start.3 = ((bf16[8,16,256]{2,1,0:T(8,128)(2,1)}), bf16[8,16,256]{2,1,0:T(8,128)(2,1)S(1)}, u32[]{:S(2)}, u32[]{:S(2)}) async-start(bf16[8,16,256]{2,1,0:T(8,128)(2,1)} %bitcast.5), calls=%async_computation.3 | async-start | bytes 131072 | tf_op jit(solution)/shard_map/all_to_all | solution.py:339
  52.1 0.6 copy-start.1
  52.7 11.5 %all-to-all-start.2 = ((bf16[16,8,256]{2,1,0:T(8,128)(2,1)}), bf16[16,8,256]{2,1,0:T(8,128)(2,1)S(1)}, u32[]{:S(2)}, u32[]{:S(2)}) async-start(bf16[16,8,256]{2,1,0:T(8,128)(2,1)} %bitcast.4), calls=%async_computation.2 | async-start | bytes 131072 | tf_op jit(solution)/shard_map/all_to_all | solution.py:354
  64.2 0.6 copy-start.2

commit v2 on v1

v2 whole, which is shorter than its diff:
```python
import jax
import jax.numpy as jnp
from jax import lax
from jax.experimental import pallas as pl
from jax.experimental.pallas import tpu as pltpu
from jax.sharding import PartitionSpec as P

F32 = jnp.float32
BF16 = jnp.bfloat16
ROWS = 8
COLS = 16
TR = 16
TC = 8
LINE = 128
D = 256
HEADS = 16
HEAD_DIM = 16
STATE = 128


def iota(shape, dim):
    return lax.broadcasted_iota(jnp.int32, shape, dim)


def halves(x):
    high = x.astype(BF16).astype(F32)
    return high, x - high


def silu(x):
    return x * jax.nn.sigmoid(x)


def pack_row_kernel(trace_ref, latent_ref, logs_ref, horizon_ref, out_ref, meta_ref, own_ref):
    r = lax.axis_index("row")
    c = lax.axis_index("col")
    own_ref[...] = latent_ref[...]
    target = iota((LINE, LINE), 0)
    source = iota((LINE, LINE), 1)
    pick = ((target % TR) * TC + target // TR == source).astype(BF16)
    flat = latent_ref[...].astype(F32).reshape(LINE, D).astype(BF16)
    columns = jnp.dot(pick, flat, preferred_element_type=F32).astype(BF16)
    halo = jnp.concatenate(
        [latent_ref[0].astype(F32), latent_ref[TR - 1].astype(F32)], axis=0
    ).astype(BF16)
    logs = jnp.where(iota((8, D), 0) == r, jnp.broadcast_to(logs_ref[...].astype(F32), (8, D)), 0.0)
    high, low = halves(horizon_ref[...])
    here = (iota((TR, LINE), 1) - TR * r == iota((TR, LINE), 0)).astype(BF16)
    lines = jnp.concatenate(
        [
            jnp.dot(high.astype(BF16), here, preferred_element_type=F32),
            jnp.dot(low.astype(BF16), here, preferred_element_type=F32),
        ],
        axis=1,
    )
    meta = jnp.concatenate([logs, lines], axis=0).astype(BF16)
    for dest in range(ROWS):
        out_ref[dest, 0:128, :] = columns
        out_ref[dest, 128:144, :] = halo
        out_ref[dest, 144:160, :] = meta
    lane = iota((TR, LINE), 1) - TC * c
    lane1 = iota((1, LINE), 1) - TC * c
    spread = jnp.zeros((TR, LINE), F32)
    trace = jnp.zeros((1, LINE), F32)
    across = horizon_ref[...].T
    for j in range(TC):
        column = jnp.broadcast_to(across[:, j : j + 1], (TR, LINE))
        spread = jnp.where(lane == j, column, spread)
        trace = jnp.where(lane1 == j, trace_ref[j].astype(F32), trace)
    high, low = halves(spread)
    first = jnp.concatenate([jnp.broadcast_to(trace, (TR, LINE)), high], axis=1)
    second = jnp.concatenate([low, jnp.zeros((TR, LINE), F32)], axis=1)
    row8 = iota((8, D), 0)
    for dest in range(COLS):
        part = jnp.where(row8 == 0, jnp.broadcast_to(first[dest : dest + 1], (8, D)), 0.0)
        part = jnp.where(row8 == 1, jnp.broadcast_to(second[dest : dest + 1], (8, D)), part)
        meta_ref[dest] = part.astype(BF16)


def pack_col_kernel(got_ref, own_ref, meta_ref, out_ref, left_ref, right_ref):
    r = lax.axis_index("row")
    above = got_ref[jnp.maximum(r - 1, 0), 128:144, :].astype(F32)[8:16]
    below = got_ref[jnp.minimum(r + 1, ROWS - 1), 128:144, :].astype(F32)[0:8]
    own = own_ref[...].astype(F32)
    logs = jnp.sum(got_ref[:, 144:160, :].astype(F32)[:, 0:8, :], axis=0)
    rows = [above] + [own[i] for i in range(TR)] + [below]
    for dest in range(COLS):
        pair = jnp.concatenate([rows[dest], rows[dest + 1]], axis=0)
        out_ref[dest, 0:16, :] = pair.astype(BF16)
        pair = jnp.concatenate([rows[dest + 2], logs], axis=0)
        out_ref[dest, 16:32, :] = pair.astype(BF16)
        out_ref[dest, 32:40, :] = meta_ref[dest]
    left_ref[...] = got_ref[:, 0:16, :]
    right_ref[...] = got_ref[:, 112:128, :]


def params_kernel(gate_ref, gain_ref, last_ref, conv_ref, bias_ref, row_ref, col_ref, wide_ref, side_ref):
    wide_ref[0:9, :] = conv_ref[...]
    wide_ref[9:10, :] = gain_ref[...]
    wide_ref[10:11, :] = last_ref[...]
    bias = bias_ref[...].T
    rates = [row_ref[...].T / 2048.0, col_ref[...].T / 2048.0]
    for k in range(4):
        side_ref[0, k * HEADS : (k + 1) * HEADS, :] = jnp.broadcast_to(
            bias[:, k : k + 1], (HEADS, LINE)
        )
        side_ref[1, k * HEADS : (k + 1) * HEADS, :] = jnp.broadcast_to(
            rates[k // 2][:, k % 2 : k % 2 + 1], (HEADS, LINE)
        )


def normalised(hidden, gain):
    scale = lax.rsqrt(jnp.mean(hidden * hidden, axis=-1, keepdims=True) + 1e-06)
    return (hidden * scale * gain).astype(BF16)


def line_scan(cells, tokens, inside, taps, gain, in_w, bc, dt_w, bias, rate, horizon, w_ref, x_ref):
    pre = []
    for s in range(3):
        n = normalised(cells[s] + tokens[s], gain)
        p = jnp.dot(n, in_w, preferred_element_type=F32).astype(BF16).astype(F32)
        pre.append(jnp.where(inside[s], p, 0.0))
    shifted = [
        taps[t][0] * pre[0] + taps[t][1] * pre[1] + taps[t][2] * pre[2] for t in range(3)
    ]
    place = iota((LINE, D), 0)
    conv = (
        shifted[1]
        + jnp.where(place == 0, 0.0, pltpu.roll(shifted[0], 1, 0))
        + jnp.where(place == LINE - 1, 0.0, pltpu.roll(shifted[2], LINE - 1, 0))
    )
    mixed = silu(conv).astype(BF16)
    coef = jnp.dot(mixed, bc, preferred_element_type=F32).astype(BF16)
    contract = (((1,), (1,)), ((), ()))
    k = iota((LINE, LINE), 0)
    j = iota((LINE, LINE), 1)
    lower = j <= k
    score_f = lax.dot_general(
        coef[:, STATE : 2 * STATE], coef[:, :STATE], contract, preferred_element_type=F32
    )
    score_b = lax.dot_general(
        coef[:, 3 * STATE :], coef[:, 2 * STATE : 3 * STATE], contract, preferred_element_type=F32
    )
    score_f = jnp.where(lower, score_f, 0.0)
    score_b = jnp.where(j >= k, score_b, 0.0)
    steps = []
    sums_t = []
    sums = []
    for side in range(2):
        z = lax.dot_general(dt_w[side], mixed, contract, preferred_element_type=F32) + bias[side]
        step = jnp.maximum(z, 0.0) + jnp.log1p(jnp.exp(-jnp.abs(z)))
        decay = -step * rate[side] - horizon
        ones = ((k <= j) if side == 0 else (k >= j)).astype(BF16)
        high, rest = halves(decay)
        middle, low = halves(rest)
        parts = jnp.concatenate([high, middle, low], axis=0).astype(BF16)
        total = jnp.dot(parts, ones, preferred_element_type=F32)
        total = total[:HEADS] + (total[HEADS : 2 * HEADS] + total[2 * HEADS :])
        steps.append(step)
        sums_t.append(total)
        sums.append(total.T)
    head_of = iota((LINE, D), 1) // HEAD_DIM
    wide = mixed.astype(F32)
    for h in range(HEADS):
        ahead = sums[0][:, h : h + 1] - sums_t[0][h : h + 1, :]
        behind = sums[1][:, h : h + 1] - sums_t[1][h : h + 1, :]
        decay = jnp.exp(jnp.where(lower, ahead, behind))
        drive = score_f * steps[0][h : h + 1, :] + score_b * steps[1][h : h + 1, :]
        w_ref[:, h * LINE : (h + 1) * LINE] = (drive * decay).astype(BF16)
        x_ref[h * LINE : (h + 1) * LINE, :] = jnp.where(head_of == h, wide, 0.0).astype(BF16)
    return jnp.dot(w_ref[...], x_ref[...], preferred_element_type=F32)


def row_kernel(
    cols_ref,
    wide_ref,
    side_ref,
    cond_ref,
    in_ref,
    bc_ref,
    dt_ref,
    out_ref,
    tokens_ref,
    w_ref,
    x_ref,
):
    r = lax.axis_index("row")
    c = lax.axis_index("col")
    pair = cols_ref[:, 0:16, :].astype(F32)
    last = cols_ref[:, 16:32, :].astype(F32)
    logs = last[:, 8:16, :].reshape(LINE, D).astype(BF16)
    tokens = silu(jnp.dot(logs, cond_ref[...], preferred_element_type=F32)).astype(BF16)
    meta = jnp.sum(cols_ref[:, 32:40, :].astype(F32), axis=0)
    trace = meta[0:1, 0:LINE].astype(jnp.int32)
    position = iota((LINE, LINE), 0)
    names = (position % ROWS) * COLS + position // ROWS
    chosen = (names == trace).astype(F32).T.astype(BF16)
    tokens = jnp.dot(chosen, tokens, preferred_element_type=F32)
    tokens_ref[...] = tokens
    row = r * TR + c
    cells = [pair[:, 0:8, :], pair[:, 8:16, :], last[:, 0:8, :]]
    cells = [x.reshape(LINE, D) for x in cells]
    out_ref[...] = line_scan(
        cells,
        [tokens, tokens, tokens],
        [row > 0, True, row < LINE - 1],
        [[wide_ref[3 * s + t : 3 * s + t + 1, :] for s in range(3)] for t in range(3)],
        wide_ref[9:10, :],
        in_ref[:, :D],
        bc_ref[:, : 4 * STATE],
        [dt_ref[:HEADS, :], dt_ref[HEADS : 2 * HEADS, :]],
        [side_ref[0, :HEADS, :], side_ref[0, HEADS : 2 * HEADS, :]],
        [side_ref[1, :HEADS, :], side_ref[1, HEADS : 2 * HEADS, :]],
        meta[0:1, LINE:] + meta[1:2, :LINE],
        w_ref,
        x_ref,
    ).astype(BF16)


def column_kernel(
    rows_ref,
    left_ref,
    right_ref,
    tokens_ref,
    own_ref,
    wide_ref,
    side_ref,
    in_ref,
    bc_ref,
    dt_ref,
    hidden_ref,
    gate_ref,
    sum_ref,
    normed_ref,
    pre_ref,
    mixed_ref,
    b_ref,
    cum_ref,
    w_ref,
    y_ref,
):
    r = lax.axis_index("row")
    c = lax.axis_index("col")
    gain = wide_ref[9:10, :]
    hidden = own_ref[...].astype(F32) + tokens_ref[pl.ds(pl.multiple_of(c * TC, TC), TC), :][None]
    hidden = hidden.reshape(LINE, D)
    hidden_ref[...] = hidden
    gate = jnp.dot(normalised(hidden, gain), in_ref[:, D:], preferred_element_type=F32)
    gate_ref[...] = silu(gate.astype(BF16).astype(F32))
    for q in range(TC + 2):
        if q == 0:
            cells = left_ref[...]
        elif q == TC + 1:
            cells = right_ref[...]
        else:
            cells = rows_ref[:, (q - 1) * TR : q * TR, :]
        line = jnp.clip(c * TC + q - 1, 0, LINE - 1)
        cells = cells.astype(F32).reshape(LINE, D) + tokens_ref[pl.ds(line, 1), :]
        normed_ref[q * LINE : (q + 1) * LINE, :] = normalised(cells, gain)
    pre_ref[...] = jnp.dot(
        normed_ref[...], in_ref[:, :D], preferred_element_type=F32
    ).astype(BF16)
    place = iota((LINE, D), 0)
    inside = [c > 0] + [True] * TC + [c < COLS - 1]
    for j in range(TC):
        pre = []
        for s in range(3):
            p = pre_ref[(j + s) * LINE : (j + s + 1) * LINE, :].astype(F32)
            pre.append(p if inside[j + s] is True else jnp.where(inside[j + s], p, 0.0))
        shifted = [
            sum(wide_ref[3 * a + s : 3 * a + s + 1, :] * pre[s] for s in range(3))
            for a in range(3)
        ]
        conv = (
            shifted[1]
            + jnp.where(place == 0, 0.0, pltpu.roll(shifted[0], 1, 0))
            + jnp.where(place == LINE - 1, 0.0, pltpu.roll(shifted[2], LINE - 1, 0))
        )
        mixed_ref[j * LINE : (j + 1) * LINE, :] = silu(conv).astype(BF16)
    base = 4 * STATE
    b_weight = jnp.concatenate(
        [bc_ref[:, base : base + STATE], bc_ref[:, base + 2 * STATE : base + 3 * STATE]], axis=1
    )
    c_weight = jnp.concatenate(
        [bc_ref[:, base + STATE : base + 2 * STATE], bc_ref[:, base + 3 * STATE :]], axis=1
    )
    b_ref[...] = jnp.dot(mixed_ref[...], b_weight, preferred_element_type=F32).astype(BF16)
    start = pl.multiple_of(r * TR, TR)
    mine = jnp.concatenate(
        [mixed_ref[pl.ds(j * LINE + start, TR), :] for j in range(TC)], axis=0
    )
    c_own = jnp.dot(mine, c_weight, preferred_element_type=F32).astype(BF16)
    contract = (((1,), (1,)), ((), ()))
    z = lax.dot_general(
        dt_ref[2 * HEADS :, :], mixed_ref[...], contract, preferred_element_type=F32
    )
    k = iota((LINE, LINE), 0)
    j_ = iota((LINE, LINE), 1)
    horizon = jnp.sum(rows_ref[:, 144:160, :].astype(F32), axis=0)[8:16]
    horizon = horizon[:, :LINE] + horizon[:, LINE:]
    steps = []
    sums = []
    for side in range(2):
        bias = side_ref[0, (2 + side) * HEADS : (3 + side) * HEADS, :]
        rate = side_ref[1, (2 + side) * HEADS : (3 + side) * HEADS, :]
        own_steps = []
        decays = []
        for j in range(TC):
            zj = z[side * HEADS : (side + 1) * HEADS, j * LINE : (j + 1) * LINE] + bias
            step = jnp.maximum(zj, 0.0) + jnp.log1p(jnp.exp(-jnp.abs(zj)))
            own_steps.append(step)
            decays.append(-step * rate - horizon[j : j + 1, :])
        decay = jnp.concatenate(decays, axis=0)
        ones = ((k <= j_) if side == 0 else (k >= j_)).astype(BF16)
        high, rest = halves(decay)
        middle, low = halves(rest)
        parts = jnp.concatenate([high, middle, low], axis=0).astype(BF16)
        total = jnp.dot(parts, ones, preferred_element_type=F32)
        total = total[:LINE] + (total[LINE : 2 * LINE] + total[2 * LINE :])
        cum_ref[side] = total.T
        steps.append(own_steps)
        sums.append(total)
    ahead_own = cum_ref[0, pl.ds(start, TR), :]
    behind_own = cum_ref[1, pl.ds(start, TR), :]
    at = iota((TR, LINE), 0) + start
    other = iota((TR, LINE), 1)
    lower = other <= at
    upper = other >= at
    head_of = iota((TR, D), 1) // HEAD_DIM
    for j in range(TC):
        cj = c_own[j * TR : (j + 1) * TR, :]
        bj = b_ref[j * LINE : (j + 1) * LINE, :]
        score_f = lax.dot_general(
            cj[:, :STATE], bj[:, :STATE], contract, preferred_element_type=F32
        )
        score_b = lax.dot_general(
            cj[:, STATE:], bj[:, STATE:], contract, preferred_element_type=F32
        )
        score_f = jnp.where(lower, score_f, 0.0)
        score_b = jnp.where(upper, score_b, 0.0)
        for h in range(HEADS):
            n = j * HEADS + h
            ahead = ahead_own[:, n : n + 1] - sums[0][n : n + 1, :]
            behind = behind_own[:, n : n + 1] - sums[1][n : n + 1, :]
            decay = jnp.exp(jnp.where(lower, ahead, behind))
            drive = score_f * steps[0][j][h : h + 1, :] + score_b * steps[1][j][h : h + 1, :]
            w_ref[j, h * TR : (h + 1) * TR, :] = (drive * decay).astype(BF16)
        full = jnp.dot(
            w_ref[j], mixed_ref[j * LINE : (j + 1) * LINE, :], preferred_element_type=F32
        )
        got = full[:TR, :]
        for h in range(1, HEADS):
            got = jnp.where(head_of == h, full[h * TR : (h + 1) * TR, :], got)
        y_ref[j * TR : (j + 1) * TR, :] = got
    pick = ((k % TC) * TR + k // TC == j_).astype(BF16)
    high, low = halves(y_ref[...])
    sum_ref[...] = jnp.dot(pick, high.astype(BF16), preferred_element_type=F32) + jnp.dot(
        pick, low.astype(BF16), preferred_element_type=F32
    )


def finish_kernel(row_ref, col_ref, hidden_ref, gate_ref, wide_ref, out_w_ref, out_ref):
    total = row_ref[...].astype(F32).reshape(LINE, D) + col_ref[...]
    scale = lax.rsqrt(jnp.mean(total * total, axis=-1, keepdims=True) + 1e-05)
    gated = (total * scale * wide_ref[10:11, :] * gate_ref[...]).astype(BF16)
    branch = jnp.dot(gated, out_w_ref[...], preferred_element_type=F32)
    out_ref[...] = (hidden_ref[...] + branch).reshape(TR, TC, D).astype(BF16)


def call(kernel, outs, *args, scratch=(), smem=0, pinned=True, result=False):
    vmem = pl.BlockSpec(memory_space=pltpu.VMEM)
    specs = [pl.BlockSpec(memory_space=pltpu.SMEM)] * smem + [vmem] * (len(args) - smem)
    if pinned is True:
        pinned = range(smem, len(args))
    args = [
        pltpu.with_memory_space_constraint(x, pltpu.VMEM) if i in pinned else x
        for i, x in enumerate(args)
    ]
    shape = jax.ShapeDtypeStruct if result else pltpu.VMEM
    return pl.pallas_call(
        kernel,
        out_shape=[shape(s, d) for s, d in outs],
        in_specs=specs,
        out_specs=[vmem] * len(outs),
        scratch_shapes=list(scratch),
        name=kernel.__name__,
    )(*args)


def per_device(
    latent,
    well_logs,
    cond_weight,
    trace_rows,
    norm_gain,
    in_weight,
    conv_weight,
    bc_weight,
    dt_weight,
    dt_bias,
    row_rate,
    col_rate,
    horizon,
    out_gain,
    out_weight,
):
    dt_weight = dt_weight.T
    packed, meta, own = call(
        pack_row_kernel,
        [((ROWS, 160, D), BF16), ((COLS, 8, D), BF16), ((TR, TC, D), BF16)],
        trace_rows,
        latent,
        well_logs,
        horizon.T,
        smem=1,
        pinned=(),
    )
    from_rows = lax.all_to_all(packed, "row", 0, 0, tiled=True)
    packed, first, last = call(
        pack_col_kernel,
        [((COLS, 40, D), BF16), ((ROWS, TR, D), BF16), ((ROWS, TR, D), BF16)],
        from_rows,
        own,
        meta,
    )
    wide, side = call(
        params_kernel,
        [((16, D), F32), ((2, 4 * HEADS, LINE), F32)],
        first,
        norm_gain.reshape(1, D),
        out_gain.reshape(1, D),
        conv_weight,
        dt_bias,
        row_rate,
        col_rate,
        pinned=(0,),
    )
    ends = COLS - 1
    right = lax.ppermute(first, "col", [(i + 1, i) for i in range(ends)])
    left = lax.ppermute(last, "col", [(i, i + 1) for i in range(ends)])
    from_cols = lax.all_to_all(packed, "col", 0, 0, tiled=True)
    by_row, tokens = call(
        row_kernel,
        [((LINE, D), BF16), ((LINE, D), F32)],
        from_cols,
        wide,
        side,
        cond_weight,
        in_weight,
        bc_weight,
        dt_weight,
        scratch=[
            pltpu.VMEM((LINE, HEADS * LINE), BF16),
            pltpu.VMEM((HEADS * LINE, D), BF16),
        ],
    )
    by_row = lax.all_to_all(by_row.reshape(COLS, TC, D), "col", 0, 0, tiled=True)
    hidden, gate, by_column = call(
        column_kernel,
        [((LINE, D), F32), ((LINE, D), F32), ((LINE, D), F32)],
        from_rows,
        left,
        right,
        tokens,
        own,
        wide,
        side,
        in_weight,
        bc_weight,
        dt_weight,
        scratch=[
            pltpu.VMEM(((TC + 2) * LINE, D), BF16),
            pltpu.VMEM(((TC + 2) * LINE, D), BF16),
            pltpu.VMEM((TC * LINE, D), BF16),
            pltpu.VMEM((TC * LINE, 2 * STATE), BF16),
            pltpu.VMEM((2, LINE, LINE), F32),
            pltpu.VMEM((TC, HEADS * TR, LINE), BF16),
            pltpu.VMEM((LINE, D), F32),
        ],
    )
    (out,) = call(
        finish_kernel,
        [((TR, TC, D), BF16)],
        by_row,
        by_column,
        hidden,
        gate,
        wide,
        out_weight,
        result=True,
    )
    return out


def solution(mesh):
    placed = (
        P("row", "col", None),
        P(("row", "col"), None),
        P(),
        P("col"),
        P(),
        P(),
        P(),
        P(),
        P(),
        P(),
        P(),
        P(),
        P("row", "col"),
        P(),
        P(),
    )
    return jax.shard_map(
        per_device, mesh=mesh, in_specs=placed, out_specs=P("row", "col", None), check_vma=False
    )
```

time: 67.7 us -> 50.8 us (0.75)
  waiting for transfers between devices: 10.5 us -> 3.1 us
  Pallas kernels: 16.2 us -> 10.4 us
  local copies, waits for them, and re-layouts: 4.06 us -> 0.02 us
  blocking collectives: 15.9 us -> 18.6 us
  starting transfers between devices: 20.2 us -> 18 us
    pallas_call x6, Pallas kernels: 16.2 us -> 10.4 us  [call(): pl.pallas_call(kernel, out_shape=[shape(s, d) for s, d in outs], in_specs...]
    unnamed x14 -> x10, local copies, waits for them, and re-layouts: 4.06 us -> 0.02 us
    all_to_all x1 -> x0, starting transfers between devices: 3.35 us -> none  [per_device(): lax.all_to_all(by_column.reshape(ROWS, TR, D), 'row', 0, 0, tiled=True)]
    all_to_all x1, blocking collectives: 15.9 us -> 18.6 us  [per_device(): from_rows = lax.all_to_all(packed, 'row', 0, 0, tiled=True)]
    all_to_all x1 -> x0, waiting for transfers between devices: 2.5 us -> none  [per_device(): lax.all_to_all(by_column.reshape(ROWS, TR, D), 'row', 0, 0, tiled=True)]
    all_to_all x1, waiting for transfers between devices: 3.9 us -> 1.81 us  [per_device(): lax.all_to_all(by_row.reshape(COLS, TC, D), 'col', 0, 0, tiled=True)]
    ppermute x1 -> x2, starting transfers between devices: 3.54 us -> 5.45 us  [the longest x1 3.53 us: per_device(): left = lax.ppermute(last, 'col', [(i, i + 1) for i in range(ends)])]
    all_to_all x1, waiting for transfers between devices: 2.76 us -> 1.28 us  [per_device(): from_cols = lax.all_to_all(packed, 'col', 0, 0, tiled=True)]
  transfers between devices with their start and end apart: 4 -> 4, of which waited for: 4 -> 2; matrix products, arithmetic and copies ran while one was open for 1% -> 0% of each run, Pallas kernels for 9% -> 15%
where the time goes in v2:
time: 50.8 us; the launch traced here: 50.3 us
  blocking collectives  18.6 us (37%)
  starting transfers between devices  18 us (35%)
  Pallas kernels  10.4 us (20%)
  waiting for transfers between devices  3.1 us (6%)
    all_to_all x1, blocking collectives, per_device(): from_rows = lax.all_to_all(packed, 'row', 0, 0, tiled=True)  18.6 us
    pallas_call x6, Pallas kernels, call(): pl.pallas_call(kernel, out_shape=[shape(s, d) for s, d in outs], in_specs...  10.4 us
    all_to_all x1, starting transfers between devices, per_device(): from_cols = lax.all_to_all(packed, 'col', 0, 0, tiled=True)  8.02 us
    all_to_all x1, starting transfers between devices, per_device(): lax.all_to_all(by_row.reshape(COLS, TC, D), 'col', 0, 0, tiled=True)  4.58 us
    ppermute x1, starting transfers between devices, per_device(): left = lax.ppermute(last, 'col', [(i, i + 1) for i in range(ends)])  3.53 us
    ppermute x1, starting transfers between devices, per_device(): right = lax.ppermute(first, 'col', [(i + 1, i) for i in range(ends)])  1.92 us
    all_to_all x1, waiting for transfers between devices, per_device(): lax.all_to_all(by_row.reshape(COLS, TC, D), 'col', 0, 0, tiled=True)  1.81 us
    all_to_all x1, waiting for transfers between devices, per_device(): from_cols = lax.all_to_all(packed, 'col', 0, 0, tiled=True)  1.28 us
  transfers between devices with their start and end apart: 4, of which 2 were waited for; matrix products, arithmetic and copies ran while one was open for 0% of the time, Pallas kernels for 15%

profile of v2, /device:TPU:1, one launch (start us, length us, event | category | flops | bytes accessed | tf_op | source)
XLA Modules:
  0.0 50.3 jit_solution(10848359493716824941)
XLA Ops:
  0.0 1.1 %pack_row_kernel.1 = (bf16[8,160,256]{2,1,0:T(8,128)(2,1)S(1)}, bf16[16,8,256]{2,1,0:T(8,128)(2,1)S(1)}, bf16[16,8,256]{2,1,0:T(8,128)(2,1)S(1)}) custom-call(s32[8]{0:T(128)} %trace_ref.1, bf16[16,8,256]{2,1,0:T(8,128)(2,1)} %latent_ref.1, bf16[1,256]{1,0:T(2,128)(2,1)} %logs_ref.1, f32[8,16]{1,0:T(8,128)} %bitcast.7), custom_call_target="tpu_custom_call" | custom-call | tf_op jit(solution)/shard_map/pack_row_kernel/pallas_call | solution.py:380
  1.1 18.6 %all_to_all.15.got_ref.rows_ref = bf16[8,160,256]{2,1,0:T(8,128)(2,1)S(1)} all-to-all(bf16[8,160,256]{2,1,0:T(8,128)(2,1)S(1)} %get-tuple-element.18), channel_id=1, replica_groups=mesh['row'=8,'col'=16] {'row'}, dimensions={0} | all-to-all | bytes 1310720 | tf_op jit(solution)/shard_map/all_to_all | solution.py:418
  19.7 0.0 copy-start.1
  19.7 0.7 %pack_col_kernel.1 = (bf16[16,40,256]{2,1,0:T(8,128)(2,1)}, bf16[8,16,256]{2,1,0:T(8,128)(2,1)S(1)}, bf16[8,16,256]{2,1,0:T(8,128)(2,1)S(1)}) custom-call(bf16[8,160,256]{2,1,0:T(8,128)(2,1)S(1)} %all_to_all.15.got_ref.rows_ref, bf16[16,8,256]{2,1,0:T(8,128)(2,1)S(1)} %get-tuple-element.19.own_ref, bf16[16,8,256]{2,1,0:T(8,128)(2,1)S(1)} %get-tuple-element.20.meta_ref), custom_call_target="tpu_custom_call" | custom-call | tf_op jit(solution)/shard_map/pack_col_kernel/pallas_call | solution.py:380
  20.4 0.0 copy-start
  20.4 8.0 %all-to-all-start.1 = ((bf16[16,40,256]{2,1,0:T(8,128)(2,1)}), bf16[16,40,256]{2,1,0:T(8,128)(2,1)S(1)}, u32[]{:S(2)}, u32[]{:S(2)}) async-start(bf16[16,40,256]{2,1,0:T(8,128)(2,1)} %get-tuple-element.21), calls=%async_computation.1 | async-start | bytes 655360 | tf_op jit(solution)/shard_map/all_to_all | solution.py:441
  28.5 3.5 %collective-permute-start = (bf16[8,16,256]{2,1,0:T(8,128)(2,1)S(1)}, bf16[8,16,256]{2,1,0:T(8,128)(2,1)S(1)}, u32[]{:S(2)}, u32[]{:S(2)}) collective-permute-start(bf16[8,16,256]{2,1,0:T(8,128)(2,1)S(1)} %get-tuple-element.26), channel_id=1, source_target_pairs={{0,1},{1,2},{2,3},{3,4},{4,5},{5,6},{6,7},{7,8},{8,9},{9,10},{10,1... | collective-permute-start | bytes 196616 | tf_op jit(solution)/shard_map/ppermute | solution.py:440
  32.0 1.9 %collective-permute-start.1 = (bf16[8,16,256]{2,1,0:T(8,128)(2,1)S(1)}, bf16[8,16,256]{2,1,0:T(8,128)(2,1)S(1)}, u32[]{:S(2)}, u32[]{:S(2)}) collective-permute-start(bf16[8,16,256]{2,1,0:T(8,128)(2,1)S(1)} %get-tuple-element.22.gate_ref), channel_id=1, source_target_pairs={{1,0},{2,1},{3,2},{4,3},{5,4},{6,5},{7,6},{8,7},{9,8},{10,9},{11,1... | collective-permute-start | bytes 196616 | tf_op jit(solution)/shard_map/ppermute | solution.py:439
  33.9 0.0 copy-start.2
  33.9 0.9 %params_kernel.1 = (f32[16,256]{1,0:T(8,128)S(1)}, f32[2,64,128]{2,1,0:T(8,128)S(1)}) custom-call(bf16[8,16,256]{2,1,0:T(8,128)(2,1)S(1)} %get-tuple-element.22.gate_ref, f32[1,256]{1,0:T(1,128)} %bitcast.8, f32[1,256]{1,0:T(1,128)} %bitcast.9, f32[9,256]{1,0:T(8,128)} %conv_ref.1, f32[4,16]{1,0:T(4,128)} %bias_ref.1, f32[2,16]{1,0:T(2,128)} %row_ref.1, ...), custom_call_target="tpu_custom_call" | custom-call | tf_op jit(solution)/shard_map/params_kernel/pallas_call | solution.py:380
  34.9 1.3 %all-to-all-done.1.cols_ref = bf16[16,40,256]{2,1,0:T(8,128)(2,1)S(1)} async-done(((bf16[16,40,256]{2,1,0:T(8,128)(2,1)}), bf16[16,40,256]{2,1,0:T(8,128)(2,1)S(1)}, u32[]{:S(2)}, u32[]{:S(2)}) %all-to-all-start.1) | async-done | bytes 327712 | tf_op jit(solution)/shard_map/all_to_all | solution.py:441
  36.1 0.0 copy-done.1
  36.1 0.0 copy-done
  36.1 0.0 copy-done.4
  36.1 0.0 copy-done.2
  36.2 2.9 %row_kernel.1 = (bf16[128,256]{1,0:T(8,128)(2,1)}, f32[128,256]{1,0:T(8,128)S(1)}) custom-call(bf16[16,40,256]{2,1,0:T(8,128)(2,1)S(1)} %all-to-all-done.1.cols_ref, f32[16,256]{1,0:T(8,128)S(1)} %get-tuple-element.23.wide_ref, f32[2,64,128]{2,1,0:T(8,128)S(1)} %get-tuple-element.24.side_ref, bf16[256,256]{1,0:T(8,128)(2,1)S(1)} %copy-done.4, ...), custom_call_target="tpu_custom_call" | custom-call | tf_op jit(solution)/shard_map/row_kernel/pallas_call | solution.py:380
  39.0 4.6 %all-to-all-start.2 = ((bf16[16,8,256]{2,1,0:T(8,128)(2,1)}), bf16[16,8,256]{2,1,0:T(8,128)(2,1)S(1)}, u32[]{:S(2)}, u32[]{:S(2)}) async-start(bf16[16,8,256]{2,1,0:T(8,128)(2,1)} %bitcast.4), calls=%async_computation.2 | async-start | bytes 131072 | tf_op jit(solution)/shard_map/all_to_all | solution.py:457
  43.6 0.0 collective-permute-done.left_ref
  43.6 0.0 collective-permute-done.1.right_ref
  43.6 0.0 copy-start.3
  43.6 4.0 %column_kernel.1 = (f32[128,256]{1,0:T(8,128)S(1)}, f32[128,256]{1,0:T(8,128)S(1)}, f32[128,256]{1,0:T(8,128)S(1)}) custom-call(bf16[8,160,256]{2,1,0:T(8,128)(2,1)S(1)} %all_to_all.15.got_ref.rows_ref, bf16[8,16,256]{2,1,0:T(8,128)(2,1)S(1)} %collective-permute-done.left_ref, bf16[8,16,256]{2,1,0:T(8,128)(2,1)S(1)} %collective-permute-done.1.right_ref, ...), custom_call_target="tpu_custom_call" | custom-call | tf_op jit(solution)/shard_map/column_kernel/pallas_call | solution.py:380
  47.6 1.8 %all-to-all-done.2.row_ref = bf16[16,8,256]{2,1,0:T(8,128)(2,1)S(1)} async-done(((bf16[16,8,256]{2,1,0:T(8,128)(2,1)}), bf16[16,8,256]{2,1,0:T(8,128)(2,1)S(1)}, u32[]{:S(2)}, u32[]{:S(2)}) %all-to-all-start.2) | async-done | bytes 65568 | tf_op jit(solution)/shard_map/all_to_all | solution.py:457
  49.4 0.0 copy-done.3
  49.4 0.9 %finish_kernel.1 = bf16[16,8,256]{2,1,0:T(8,128)(2,1)} custom-call(bf16[16,8,256]{2,1,0:T(8,128)(2,1)S(1)} %all-to-all-done.2.row_ref, f32[128,256]{1,0:T(8,128)S(1)} %get-tuple-element.28.col_ref, f32[128,256]{1,0:T(8,128)S(1)} %get-tuple-element.29.hidden_ref, f32[128,256]{1,0:T(8,128)S(1)} %get-tuple-element.30.gate_ref, ...), custom_call_target="tpu_custom_call" | custom-call | tf_op jit(solution)/shard_map/finish_kernel/pallas_call | solution.py:380
  (1 shorter events, 0.0 us)
Async XLA Ops:
  19.7 16.5 %copy-start.1 = (bf16[256,512]{1,0:T(8,128)(2,1)S(1)}, bf16[256,512]{1,0:T(8,128)(2,1)}, u32[]{:S(2)}) copy-start(bf16[256,512]{1,0:T(8,128)(2,1)} %in_ref.3) | copy-start | bytes 786436
  20.4 15.7 %copy-start = (bf16[256,1024]{1,0:T(8,128)(2,1)S(1)}, bf16[256,1024]{1,0:T(8,128)(2,1)}, u32[]{:S(2)}) copy-start(bf16[256,1024]{1,0:T(8,128)(2,1)} %bc_ref.3) | copy-start | bytes 1572868
  20.4 15.7 %copy-start.4 = (bf16[256,256]{1,0:T(8,128)(2,1)S(1)}, bf16[256,256]{1,0:T(8,128)(2,1)}, u32[]{:S(2)}) copy-start(bf16[256,256]{1,0:T(8,128)(2,1)} %cond_ref.1) | copy-start | bytes 393220
  20.4 15.7 %all-to-all-start.1 = ((bf16[16,40,256]{2,1,0:T(8,128)(2,1)}), bf16[16,40,256]{2,1,0:T(8,128)(2,1)S(1)}, u32[]{:S(2)}, u32[]{:S(2)}) async-start(bf16[16,40,256]{2,1,0:T(8,128)(2,1)} %get-tuple-element.21), calls=%async_computation.1 | async-start | bytes 655360 | tf_op jit(solution)/shard_map/all_to_all | solution.py:441
  28.5 15.2 %collective-permute-start = (bf16[8,16,256]{2,1,0:T(8,128)(2,1)S(1)}, bf16[8,16,256]{2,1,0:T(8,128)(2,1)S(1)}, u32[]{:S(2)}, u32[]{:S(2)}) collective-permute-start(bf16[8,16,256]{2,1,0:T(8,128)(2,1)S(1)} %get-tuple-element.26), channel_id=1, source_target_pairs={{0,1},{1,2},{2,3},{3,4},{4,5},{5,6},{6,7},{7,8},{8,9},{9,10},{10,1... | collective-permute-start | bytes 196616 | tf_op jit(solution)/shard_map/ppermute | solution.py:440
  32.0 11.6 %collective-permute-start.1 = (bf16[8,16,256]{2,1,0:T(8,128)(2,1)S(1)}, bf16[8,16,256]{2,1,0:T(8,128)(2,1)S(1)}, u32[]{:S(2)}, u32[]{:S(2)}) collective-permute-start(bf16[8,16,256]{2,1,0:T(8,128)(2,1)S(1)} %get-tuple-element.22.gate_ref), channel_id=1, source_target_pairs={{1,0},{2,1},{3,2},{4,3},{5,4},{6,5},{7,6},{8,7},{9,8},{10,9},{11,1... | collective-permute-start | bytes 196616 | tf_op jit(solution)/shard_map/ppermute | solution.py:439
  33.9 2.2 %copy-start.2 = (bf16[256,64]{0,1:T(8,128)(2,1)S(1)}, bf16[256,64]{0,1:T(8,128)(2,1)}, u32[]{:S(2)}) copy-start(bf16[256,64]{0,1:T(8,128)(2,1)} %param.23) | copy-start | bytes 98308
  39.0 10.4 %all-to-all-start.2 = ((bf16[16,8,256]{2,1,0:T(8,128)(2,1)}), bf16[16,8,256]{2,1,0:T(8,128)(2,1)S(1)}, u32[]{:S(2)}, u32[]{:S(2)}) async-start(bf16[16,8,256]{2,1,0:T(8,128)(2,1)} %bitcast.4), calls=%async_computation.2 | async-start | bytes 131072 | tf_op jit(solution)/shard_map/all_to_all | solution.py:457
  43.6 5.8 %copy-start.3 = (bf16[256,256]{1,0:T(8,128)(2,1)S(1)}, bf16[256,256]{1,0:T(8,128)(2,1)}, u32[]{:S(2)}) copy-start(bf16[256,256]{1,0:T(8,128)(2,1)} %out_w_ref.1) | copy-start | bytes 393220

commit v3 on v2

--- a/solution.py
+++ b/solution.py
@@ -31,33 +31,51 @@
     return x * jax.nn.sigmoid(x)
 
 
-def pack_row_kernel(trace_ref, latent_ref, logs_ref, horizon_ref, out_ref, meta_ref, own_ref):
+def pack_row_kernel(
+    trace_ref,
+    latent_ref,
+    logs_ref,
+    horizon_ref,
+    gain_ref,
+    last_ref,
+    conv_ref,
+    bias_ref,
+    row_ref,
+    col_ref,
+    out_ref,
+    meta_ref,
+    own_ref,
+    wide_ref,
+    side_ref,
+):
     r = lax.axis_index("row")
     c = lax.axis_index("col")
     own_ref[...] = latent_ref[...]
     target = iota((LINE, LINE), 0)
     source = iota((LINE, LINE), 1)
-    pick = ((target % TR) * TC + target // TR == source).astype(BF16)
+    pick = ((target & (TR - 1)) * TC + (target >> 4) == source).astype(BF16)
     flat = latent_ref[...].astype(F32).reshape(LINE, D).astype(BF16)
     columns = jnp.dot(pick, flat, preferred_element_type=F32).astype(BF16)
-    halo = jnp.concatenate(
-        [latent_ref[0].astype(F32), latent_ref[TR - 1].astype(F32)], axis=0
-    ).astype(BF16)
-    logs = jnp.where(iota((8, D), 0) == r, jnp.broadcast_to(logs_ref[...].astype(F32), (8, D)), 0.0)
     high, low = halves(horizon_ref[...])
-    here = (iota((TR, LINE), 1) - TR * r == iota((TR, LINE), 0)).astype(BF16)
-    lines = jnp.concatenate(
-        [
-            jnp.dot(high.astype(BF16), here, preferred_element_type=F32),
-            jnp.dot(low.astype(BF16), here, preferred_element_type=F32),
-        ],
-        axis=1,
-    )
-    meta = jnp.concatenate([logs, lines], axis=0).astype(BF16)
+    place = iota((TR, LINE), 1)
+    cell = iota((TR, LINE), 0)
+    first = (place - TR * r == cell).astype(BF16)
+    second = (place - ((TR * r + LINE // 2) & (LINE - 1)) == cell).astype(BF16)
+    lines = jnp.dot(high.astype(BF16), first, preferred_element_type=F32) + jnp.dot(
+        low.astype(BF16), second, preferred_element_type=F32
+    )
+    log = logs_ref[...].astype(F32)
+    row8 = iota((8, LINE), 0)
+    log = jnp.where(
+        row8 == 0,
+        jnp.broadcast_to(log[:, :LINE], (8, LINE)),
+        jnp.broadcast_to(log[:, LINE:], (8, LINE)),
+    )
+    extra = jnp.concatenate([lines, log], axis=0).astype(BF16)
     for dest in range(ROWS):
-        out_ref[dest, 0:128, :] = columns
-        out_ref[dest, 128:144, :] = halo
-        out_ref[dest, 144:160, :] = meta
+        for j in range(TC):
+            out_ref[dest, :, j * D : (j + 1) * D] = columns[j * TR : (j + 1) * TR, :]
+        out_ref[dest, :, TC * D :] = extra
     lane = iota((TR, LINE), 1) - TC * c
     lane1 = iota((1, LINE), 1) - TC * c
     spread = jnp.zeros((TR, LINE), F32)
@@ -68,33 +86,12 @@
         spread = jnp.where(lane == j, column, spread)
         trace = jnp.where(lane1 == j, trace_ref[j].astype(F32), trace)
     high, low = halves(spread)
-    first = jnp.concatenate([jnp.broadcast_to(trace, (TR, LINE)), high], axis=1)
-    second = jnp.concatenate([low, jnp.zeros((TR, LINE), F32)], axis=1)
-    row8 = iota((8, D), 0)
+    row8 = iota((8, LINE), 0)
     for dest in range(COLS):
-        part = jnp.where(row8 == 0, jnp.broadcast_to(first[dest : dest + 1], (8, D)), 0.0)
-        part = jnp.where(row8 == 1, jnp.broadcast_to(second[dest : dest + 1], (8, D)), part)
+        part = jnp.where(row8 == 0, jnp.broadcast_to(trace, (8, LINE)), 0.0)
+        part = jnp.where(row8 == 1, jnp.broadcast_to(high[dest : dest + 1], (8, LINE)), part)
+        part = jnp.where(row8 == 2, jnp.broadcast_to(low[dest : dest + 1], (8, LINE)), part)
         meta_ref[dest] = part.astype(BF16)
-
-
-def pack_col_kernel(got_ref, own_ref, meta_ref, out_ref, left_ref, right_ref):
-    r = lax.axis_index("row")
-    above = got_ref[jnp.maximum(r - 1, 0), 128:144, :].astype(F32)[8:16]
-    below = got_ref[jnp.minimum(r + 1, ROWS - 1), 128:144, :].astype(F32)[0:8]
-    own = own_ref[...].astype(F32)
-    logs = jnp.sum(got_ref[:, 144:160, :].astype(F32)[:, 0:8, :], axis=0)
-    rows = [above] + [own[i] for i in range(TR)] + [below]
-    for dest in range(COLS):
-        pair = jnp.concatenate([rows[dest], rows[dest + 1]], axis=0)
-        out_ref[dest, 0:16, :] = pair.astype(BF16)
-        pair = jnp.concatenate([rows[dest + 2], logs], axis=0)
-        out_ref[dest, 16:32, :] = pair.astype(BF16)
-        out_ref[dest, 32:40, :] = meta_ref[dest]
-    left_ref[...] = got_ref[:, 0:16, :]
-    right_ref[...] = got_ref[:, 112:128, :]
-
-
-def params_kernel(gate_ref, gain_ref, last_ref, conv_ref, bias_ref, row_ref, col_ref, wide_ref, side_ref):
     wide_ref[0:9, :] = conv_ref[...]
     wide_ref[9:10, :] = gain_ref[...]
     wide_ref[10:11, :] = last_ref[...]
@@ -109,17 +106,44 @@
         )
 
 
+def pack_col_kernel(got_ref, own_ref, meta_ref, out_ref, left_ref, right_ref):
+    r = lax.axis_index("row")
+    up = got_ref[jnp.maximum(r - 1, 0)].astype(F32)[TR - 1 : TR, :]
+    down = got_ref[jnp.minimum(r + 1, ROWS - 1)].astype(F32)[0:1, :]
+    above = jnp.concatenate([up[:, j * D : (j + 1) * D] for j in range(TC)], axis=0)
+    below = jnp.concatenate([down[:, j * D : (j + 1) * D] for j in range(TC)], axis=0)
+    own = own_ref[...].astype(F32)
+    extra = got_ref[:, :, TC * D :].astype(F32)
+    logs = jnp.concatenate(
+        [
+            jnp.concatenate([extra[s, 8 + half : 9 + half, :] for s in range(ROWS)], axis=0)
+            for half in range(2)
+        ],
+        axis=1,
+    )
+    rows = [above] + [own[i] for i in range(TR)] + [below]
+    rows = [x.astype(BF16) for x in rows]
+    logs = logs.astype(BF16)
+    for dest in range(COLS):
+        for slot in range(3):
+            out_ref[dest, :, slot * D : (slot + 1) * D] = rows[dest + slot]
+        out_ref[dest, :, 3 * D : 4 * D] = logs
+        out_ref[dest, :, 4 * D :] = meta_ref[dest]
+    left_ref[...] = got_ref[:, :, 0:D]
+    right_ref[...] = got_ref[:, :, (TC - 1) * D : TC * D]
+
+
 def normalised(hidden, gain):
     scale = lax.rsqrt(jnp.mean(hidden * hidden, axis=-1, keepdims=True) + 1e-06)
     return (hidden * scale * gain).astype(BF16)
 
 
 def line_scan(cells, tokens, inside, taps, gain, in_w, bc, dt_w, bias, rate, horizon, w_ref, x_ref):
-    pre = []
-    for s in range(3):
-        n = normalised(cells[s] + tokens[s], gain)
-        p = jnp.dot(n, in_w, preferred_element_type=F32).astype(BF16).astype(F32)
-        pre.append(jnp.where(inside[s], p, 0.0))
+    n = jnp.concatenate([normalised(cells[s] + tokens[s], gain) for s in range(3)], axis=0)
+    p = jnp.dot(n, in_w, preferred_element_type=F32).astype(BF16).astype(F32)
+    pre = [
+        jnp.where(inside[s], p[s * LINE : (s + 1) * LINE, :], 0.0) for s in range(3)
+    ]
     shifted = [
         taps[t][0] * pre[0] + taps[t][1] * pre[1] + taps[t][2] * pre[2] for t in range(3)
     ]
@@ -143,22 +167,22 @@
     )
     score_f = jnp.where(lower, score_f, 0.0)
     score_b = jnp.where(j >= k, score_b, 0.0)
+    z = lax.dot_general(dt_w, mixed, contract, preferred_element_type=F32) + bias
+    step = jnp.maximum(z, 0.0) + jnp.log1p(jnp.exp(-jnp.abs(z)))
+    decay = -step * rate - horizon
+    high, rest = halves(decay)
+    middle, low = halves(rest)
     steps = []
     sums_t = []
-    sums = []
     for side in range(2):
-        z = lax.dot_general(dt_w[side], mixed, contract, preferred_element_type=F32) + bias[side]
-        step = jnp.maximum(z, 0.0) + jnp.log1p(jnp.exp(-jnp.abs(z)))
-        decay = -step * rate[side] - horizon
+        at = slice(side * HEADS, (side + 1) * HEADS)
+        steps.append(step[at])
         ones = ((k <= j) if side == 0 else (k >= j)).astype(BF16)
-        high, rest = halves(decay)
-        middle, low = halves(rest)
-        parts = jnp.concatenate([high, middle, low], axis=0).astype(BF16)
+        parts = jnp.concatenate([high[at], middle[at], low[at]], axis=0).astype(BF16)
         total = jnp.dot(parts, ones, preferred_element_type=F32)
         total = total[:HEADS] + (total[HEADS : 2 * HEADS] + total[2 * HEADS :])
-        steps.append(step)
         sums_t.append(total)
-        sums.append(total.T)
+    sums = [x.T for x in sums_t]
     head_of = iota((LINE, D), 1) // HEAD_DIM
     wide = mixed.astype(F32)
     for h in range(HEADS):
@@ -186,20 +210,19 @@
 ):
     r = lax.axis_index("row")
     c = lax.axis_index("col")
-    pair = cols_ref[:, 0:16, :].astype(F32)
-    last = cols_ref[:, 16:32, :].astype(F32)
-    logs = last[:, 8:16, :].reshape(LINE, D).astype(BF16)
+    logs = cols_ref[:, :, 3 * D : 4 * D].astype(F32).reshape(LINE, D).astype(BF16)
     tokens = silu(jnp.dot(logs, cond_ref[...], preferred_element_type=F32)).astype(BF16)
-    meta = jnp.sum(cols_ref[:, 32:40, :].astype(F32), axis=0)
-    trace = meta[0:1, 0:LINE].astype(jnp.int32)
-    position = iota((LINE, LINE), 0)
-    names = (position % ROWS) * COLS + position // ROWS
-    chosen = (names == trace).astype(F32).T.astype(BF16)
+    meta = jnp.sum(cols_ref[:, :, 4 * D :].astype(F32), axis=0)
+    trace = jnp.broadcast_to(meta[0:1, :], (8, LINE)).T[:, 0:1].astype(jnp.int32)
+    position = iota((1, LINE), 1)
+    names = (position & (ROWS - 1)) * COLS + (position >> 3)
+    chosen = (names == trace).astype(BF16)
     tokens = jnp.dot(chosen, tokens, preferred_element_type=F32)
     tokens_ref[...] = tokens
     row = r * TR + c
-    cells = [pair[:, 0:8, :], pair[:, 8:16, :], last[:, 0:8, :]]
-    cells = [x.reshape(LINE, D) for x in cells]
+    cells = [
+        cols_ref[:, :, s * D : (s + 1) * D].astype(F32).reshape(LINE, D) for s in range(3)
+    ]
     out_ref[...] = line_scan(
         cells,
         [tokens, tokens, tokens],
@@ -208,10 +231,10 @@
         wide_ref[9:10, :],
         in_ref[:, :D],
         bc_ref[:, : 4 * STATE],
-        [dt_ref[:HEADS, :], dt_ref[HEADS : 2 * HEADS, :]],
-        [side_ref[0, :HEADS, :], side_ref[0, HEADS : 2 * HEADS, :]],
-        [side_ref[1, :HEADS, :], side_ref[1, HEADS : 2 * HEADS, :]],
-        meta[0:1, LINE:] + meta[1:2, :LINE],
+        dt_ref[: 2 * HEADS, :],
+        side_ref[0, : 2 * HEADS, :],
+        side_ref[1, : 2 * HEADS, :],
+        meta[1:2, :] + meta[2:3, :],
         w_ref,
         x_ref,
     ).astype(BF16)
@@ -253,7 +276,7 @@
         elif q == TC + 1:
             cells = right_ref[...]
         else:
-            cells = rows_ref[:, (q - 1) * TR : q * TR, :]
+            cells = rows_ref[:, :, (q - 1) * D : q * D]
         line = jnp.clip(c * TC + q - 1, 0, LINE - 1)
         cells = cells.astype(F32).reshape(LINE, D) + tokens_ref[pl.ds(line, 1), :]
         normed_ref[q * LINE : (q + 1) * LINE, :] = normalised(cells, gain)
@@ -296,8 +319,14 @@
     )
     k = iota((LINE, LINE), 0)
     j_ = iota((LINE, LINE), 1)
-    horizon = jnp.sum(rows_ref[:, 144:160, :].astype(F32), axis=0)[8:16]
-    horizon = horizon[:, :LINE] + horizon[:, LINE:]
+    extra = rows_ref[:, :, TC * D :].astype(F32)
+    owner = iota((TC, LINE), 1) >> 4
+    high = jnp.zeros((TC, LINE), F32)
+    low = jnp.zeros((TC, LINE), F32)
+    for s in range(ROWS):
+        high = jnp.where(owner == s, extra[s, :TC, :], high)
+        low = jnp.where(owner == (s + ROWS // 2) % ROWS, extra[s, :TC, :], low)
+    horizon = high + pltpu.roll(low, LINE // 2, 1)
     steps = []
     sums = []
     for side in range(2):
@@ -405,35 +434,35 @@
     out_weight,
 ):
     dt_weight = dt_weight.T
-    packed, meta, own = call(
+    packed, meta, own, wide, side = call(
         pack_row_kernel,
-        [((ROWS, 160, D), BF16), ((COLS, 8, D), BF16), ((TR, TC, D), BF16)],
+        [
+            ((ROWS, TR, TC * D + LINE), BF16),
+            ((COLS, 8, LINE), BF16),
+            ((TR, TC, D), BF16),
+            ((16, D), F32),
+            ((2, 4 * HEADS, LINE), F32),
+        ],
         trace_rows,
         latent,
         well_logs,
         horizon.T,
-        smem=1,
-        pinned=(),
-    )
-    from_rows = lax.all_to_all(packed, "row", 0, 0, tiled=True)
-    packed, first, last = call(
-        pack_col_kernel,
-        [((COLS, 40, D), BF16), ((ROWS, TR, D), BF16), ((ROWS, TR, D), BF16)],
-        from_rows,
-        own,
-        meta,
-    )
-    wide, side = call(
-        params_kernel,
-        [((16, D), F32), ((2, 4 * HEADS, LINE), F32)],
-        first,
         norm_gain.reshape(1, D),
         out_gain.reshape(1, D),
         conv_weight,
         dt_bias,
         row_rate,
         col_rate,
-        pinned=(0,),
+        smem=1,
+        pinned=(),
+    )
+    from_rows = lax.all_to_all(packed, "row", 0, 0, tiled=True)
+    packed, first, last = call(
+        pack_col_kernel,
+        [((COLS, 8, 4 * D + LINE), BF16), ((ROWS, TR, D), BF16), ((ROWS, TR, D), BF16)],
+        from_rows,
+        own,
+        meta,
     )
     ends = COLS - 1
     right = lax.ppermute(first, "col", [(i + 1, i) for i in range(ends)])

time: 50.8 us -> 49.5 us (0.974)
  Pallas kernels: 10.4 us -> 9.51 us
  waiting for transfers between devices: 3.1 us -> 3.79 us
    pallas_call x6 -> x5, Pallas kernels: 10.4 us -> 9.51 us  [call(): pl.pallas_call(kernel, out_shape=[shape(s, d) for s, d in outs], in_specs...]
    all_to_all x1, waiting for transfers between devices: 1.28 us -> 1.93 us  [per_device(): from_cols = lax.all_to_all(packed, 'col', 0, 0, tiled=True)]
  transfers between devices with their start and end apart: 4 -> 4, of which waited for: 2 -> 2; matrix products, arithmetic and copies ran while one was open for 0% -> 0% of each run, Pallas kernels for 15% -> 14%
where the time goes in v3:
time: 49.5 us; the launch traced here: 49.1 us
  blocking collectives  18.1 us (37%)
  starting transfers between devices  17.6 us (36%)
  Pallas kernels  9.51 us (19%)
  waiting for transfers between devices  3.79 us (8%)
    all_to_all x1, blocking collectives, per_device(): from_rows = lax.all_to_all(packed, 'row', 0, 0, tiled=True)  18.1 us
    pallas_call x5, Pallas kernels, call(): pl.pallas_call(kernel, out_shape=[shape(s, d) for s, d in outs], in_specs...  9.51 us
    all_to_all x1, starting transfers between devices, per_device(): from_cols = lax.all_to_all(packed, 'col', 0, 0, tiled=True)  7.76 us
    all_to_all x1, starting transfers between devices, per_device(): lax.all_to_all(by_row.reshape(COLS, TC, D), 'col', 0, 0, tiled=True)  4.4 us
    ppermute x1, starting transfers between devices, per_device(): left = lax.ppermute(last, 'col', [(i, i + 1) for i in range(ends)])  3.53 us
    all_to_all x1, waiting for transfers between devices, per_device(): from_cols = lax.all_to_all(packed, 'col', 0, 0, tiled=True)  1.93 us
    ppermute x1, starting transfers between devices, per_device(): right = lax.ppermute(first, 'col', [(i + 1, i) for i in range(ends)])  1.92 us
    all_to_all x1, waiting for transfers between devices, per_device(): lax.all_to_all(by_row.reshape(COLS, TC, D), 'col', 0, 0, tiled=True)  1.86 us
  transfers between devices with their start and end apart: 4, of which 2 were waited for; matrix products, arithmetic and copies ran while one was open for 0% of the time, Pallas kernels for 14%

profile of v3, /device:TPU:1, one launch (start us, length us, event | category | flops | bytes accessed | tf_op | source)
XLA Modules:
  0.0 49.1 jit_solution(10164778611353560835)
XLA Ops:
  0.0 1.1 %pack_row_kernel.1 = (bf16[8,16,2176]{2,1,0:T(8,128)(2,1)S(1)}, bf16[16,8,128]{2,1,0:T(8,128)(2,1)S(1)}, bf16[16,8,256]{2,1,0:T(8,128)(2,1)S(1)}, f32[16,256]{1,0:T(8,128)S(1)}, f32[2,64,128]{2,1,0:T(8,128)S(1)}) custom-call(s32[8]{0:T(128)} %trace_ref.1, bf16[16,8,256]{2,1,0:T(8,128)(2,1)} %latent_ref.1, bf16[1,256]{1,0:T(2,128)(2,1)} %logs_ref.1, ...), custom_call_target="tpu_custom_call" | custom-call | tf_op jit(solution)/shard_map/pack_row_kernel/pallas_call | solution.py:409
  1.1 18.1 %all_to_all.15.got_ref.rows_ref = bf16[8,16,2176]{2,1,0:T(8,128)(2,1)S(1)} all-to-all(bf16[8,16,2176]{2,1,0:T(8,128)(2,1)S(1)} %get-tuple-element.18), channel_id=1, replica_groups=mesh['row'=8,'col'=16] {'row'}, dimensions={0} | all-to-all | bytes 1114112 | tf_op jit(solution)/shard_map/all_to_all | solution.py:459
  19.3 0.0 copy-start
  19.3 0.8 %pack_col_kernel.1 = (bf16[16,8,1152]{2,1,0:T(8,128)(2,1)}, bf16[8,16,256]{2,1,0:T(8,128)(2,1)S(1)}, bf16[8,16,256]{2,1,0:T(8,128)(2,1)S(1)}) custom-call(bf16[8,16,2176]{2,1,0:T(8,128)(2,1)S(1)} %all_to_all.15.got_ref.rows_ref, bf16[16,8,256]{2,1,0:T(8,128)(2,1)S(1)} %get-tuple-element.19.own_ref, bf16[16,8,128]{2,1,0:T(8,128)(2,1)S(1)} %get-tuple-element.20.meta_ref), custom_call_target="tpu_custom_call" | custom-call | tf_op jit(solution)/shard_map/pack_col_kernel/pallas_call | solution.py:409
  20.0 0.0 copy-start.1
  20.0 0.0 copy-start.2
  20.0 0.0 copy-start.4
  20.0 7.8 %all-to-all-start.1 = ((bf16[16,8,1152]{2,1,0:T(8,128)(2,1)}), bf16[16,8,1152]{2,1,0:T(8,128)(2,1)S(1)}, u32[]{:S(2)}, u32[]{:S(2)}) async-start(bf16[16,8,1152]{2,1,0:T(8,128)(2,1)} %get-tuple-element.21), calls=%async_computation.1 | async-start | bytes 589824 | tf_op jit(solution)/shard_map/all_to_all | solution.py:470
  27.8 3.5 %collective-permute-start = (bf16[8,16,256]{2,1,0:T(8,128)(2,1)S(1)}, bf16[8,16,256]{2,1,0:T(8,128)(2,1)S(1)}, u32[]{:S(2)}, u32[]{:S(2)}) collective-permute-start(bf16[8,16,256]{2,1,0:T(8,128)(2,1)S(1)} %get-tuple-element.25), channel_id=1, source_target_pairs={{0,1},{1,2},{2,3},{3,4},{4,5},{5,6},{6,7},{7,8},{8,9},{9,10},{10,1... | collective-permute-start | bytes 196616 | tf_op jit(solution)/shard_map/ppermute | solution.py:469
  31.3 1.9 %collective-permute-start.1 = (bf16[8,16,256]{2,1,0:T(8,128)(2,1)S(1)}, bf16[8,16,256]{2,1,0:T(8,128)(2,1)S(1)}, u32[]{:S(2)}, u32[]{:S(2)}) collective-permute-start(bf16[8,16,256]{2,1,0:T(8,128)(2,1)S(1)} %get-tuple-element.26), channel_id=1, source_target_pairs={{1,0},{2,1},{3,2},{4,3},{5,4},{6,5},{7,6},{8,7},{9,8},{10,9},{11,1... | collective-permute-start | bytes 196616 | tf_op jit(solution)/shard_map/ppermute | solution.py:468
  33.3 1.9 %all-to-all-done.1.cols_ref = bf16[16,8,1152]{2,1,0:T(8,128)(2,1)S(1)} async-done(((bf16[16,8,1152]{2,1,0:T(8,128)(2,1)}), bf16[16,8,1152]{2,1,0:T(8,128)(2,1)S(1)}, u32[]{:S(2)}, u32[]{:S(2)}) %all-to-all-start.1) | async-done | bytes 294944 | tf_op jit(solution)/shard_map/all_to_all | solution.py:470
  35.2 0.0 copy-done
  35.2 0.0 copy-done.1
  35.2 0.0 copy-done.2
  35.2 0.0 copy-done.4
  35.2 2.8 %row_kernel.1 = (bf16[128,256]{1,0:T(8,128)(2,1)}, f32[128,256]{1,0:T(8,128)S(1)}) custom-call(bf16[16,8,1152]{2,1,0:T(8,128)(2,1)S(1)} %all-to-all-done.1.cols_ref, f32[16,256]{1,0:T(8,128)S(1)} %get-tuple-element.22.wide_ref, f32[2,64,128]{2,1,0:T(8,128)S(1)} %get-tuple-element.23.side_ref, bf16[256,256]{1,0:T(8,128)(2,1)S(1)} %copy-done.4, ...), custom_call_target="tpu_custom_call" | custom-call | tf_op jit(solution)/shard_map/row_kernel/pallas_call | solution.py:409
  38.0 4.4 %all-to-all-start.2 = ((bf16[16,8,256]{2,1,0:T(8,128)(2,1)}), bf16[16,8,256]{2,1,0:T(8,128)(2,1)S(1)}, u32[]{:S(2)}, u32[]{:S(2)}) async-start(bf16[16,8,256]{2,1,0:T(8,128)(2,1)} %bitcast.4), calls=%async_computation.2 | async-start | bytes 131072 | tf_op jit(solution)/shard_map/all_to_all | solution.py:486
  42.4 0.0 collective-permute-done.left_ref
  42.4 0.0 collective-permute-done.1.right_ref
  42.4 0.0 copy-start.3
  42.4 4.0 %column_kernel.1 = (f32[128,256]{1,0:T(8,128)S(1)}, f32[128,256]{1,0:T(8,128)S(1)}, f32[128,256]{1,0:T(8,128)S(1)}) custom-call(bf16[8,16,2176]{2,1,0:T(8,128)(2,1)S(1)} %all_to_all.15.got_ref.rows_ref, bf16[8,16,256]{2,1,0:T(8,128)(2,1)S(1)} %collective-permute-done.left_ref, bf16[8,16,256]{2,1,0:T(8,128)(2,1)S(1)} %collective-permute-done.1.right_ref, ...), custom_call_target="tpu_custom_call" | custom-call | tf_op jit(solution)/shard_map/column_kernel/pallas_call | solution.py:409
  46.4 1.9 %all-to-all-done.2.row_ref = bf16[16,8,256]{2,1,0:T(8,128)(2,1)S(1)} async-done(((bf16[16,8,256]{2,1,0:T(8,128)(2,1)}), bf16[16,8,256]{2,1,0:T(8,128)(2,1)S(1)}, u32[]{:S(2)}, u32[]{:S(2)}) %all-to-all-start.2) | async-done | bytes 65568 | tf_op jit(solution)/shard_map/all_to_all | solution.py:486
  48.3 0.0 copy-done.3
  48.3 0.9 %finish_kernel.1 = bf16[16,8,256]{2,1,0:T(8,128)(2,1)} custom-call(bf16[16,8,256]{2,1,0:T(8,128)(2,1)S(1)} %all-to-all-done.2.row_ref, f32[128,256]{1,0:T(8,128)S(1)} %get-tuple-element.28.col_ref, f32[128,256]{1,0:T(8,128)S(1)} %get-tuple-element.29.hidden_ref, f32[128,256]{1,0:T(8,128)S(1)} %get-tuple-element.30.gate_ref, ...), custom_call_target="tpu_custom_call" | custom-call | tf_op jit(solution)/shard_map/finish_kernel/pallas_call | solution.py:409
Async XLA Ops:
  19.3 15.9 %copy-start = (bf16[256,1024]{1,0:T(8,128)(2,1)S(1)}, bf16[256,1024]{1,0:T(8,128)(2,1)}, u32[]{:S(2)}) copy-start(bf16[256,1024]{1,0:T(8,128)(2,1)} %bc_ref.3) | copy-start | bytes 1572868
  20.0 15.2 %copy-start.1 = (bf16[256,512]{1,0:T(8,128)(2,1)S(1)}, bf16[256,512]{1,0:T(8,128)(2,1)}, u32[]{:S(2)}) copy-start(bf16[256,512]{1,0:T(8,128)(2,1)} %in_ref.3) | copy-start | bytes 786436
  20.0 15.2 %copy-start.2 = (bf16[256,64]{0,1:T(8,128)(2,1)S(1)}, bf16[256,64]{0,1:T(8,128)(2,1)}, u32[]{:S(2)}) copy-start(bf16[256,64]{0,1:T(8,128)(2,1)} %param.23) | copy-start | bytes 98308
  20.0 15.2 %copy-start.4 = (bf16[256,256]{1,0:T(8,128)(2,1)S(1)}, bf16[256,256]{1,0:T(8,128)(2,1)}, u32[]{:S(2)}) copy-start(bf16[256,256]{1,0:T(8,128)(2,1)} %cond_ref.1) | copy-start | bytes 393220
  20.0 15.1 %all-to-all-start.1 = ((bf16[16,8,1152]{2,1,0:T(8,128)(2,1)}), bf16[16,8,1152]{2,1,0:T(8,128)(2,1)S(1)}, u32[]{:S(2)}, u32[]{:S(2)}) async-start(bf16[16,8,1152]{2,1,0:T(8,128)(2,1)} %get-tuple-element.21), calls=%async_computation.1 | async-start | bytes 589824 | tf_op jit(solution)/shard_map/all_to_all | solution.py:470
  27.8 14.6 %collective-permute-start = (bf16[8,16,256]{2,1,0:T(8,128)(2,1)S(1)}, bf16[8,16,256]{2,1,0:T(8,128)(2,1)S(1)}, u32[]{:S(2)}, u32[]{:S(2)}) collective-permute-start(bf16[8,16,256]{2,1,0:T(8,128)(2,1)S(1)} %get-tuple-element.25), channel_id=1, source_target_pairs={{0,1},{1,2},{2,3},{3,4},{4,5},{5,6},{6,7},{7,8},{8,9},{9,10},{10,1... | collective-permute-start | bytes 196616 | tf_op jit(solution)/shard_map/ppermute | solution.py:469
  31.3 11.1 %collective-permute-start.1 = (bf16[8,16,256]{2,1,0:T(8,128)(2,1)S(1)}, bf16[8,16,256]{2,1,0:T(8,128)(2,1)S(1)}, u32[]{:S(2)}, u32[]{:S(2)}) collective-permute-start(bf16[8,16,256]{2,1,0:T(8,128)(2,1)S(1)} %get-tuple-element.26), channel_id=1, source_target_pairs={{1,0},{2,1},{3,2},{4,3},{5,4},{6,5},{7,6},{8,7},{9,8},{10,9},{11,1... | collective-permute-start | bytes 196616 | tf_op jit(solution)/shard_map/ppermute | solution.py:468
  38.0 10.3 %all-to-all-start.2 = ((bf16[16,8,256]{2,1,0:T(8,128)(2,1)}), bf16[16,8,256]{2,1,0:T(8,128)(2,1)S(1)}, u32[]{:S(2)}, u32[]{:S(2)}) async-start(bf16[16,8,256]{2,1,0:T(8,128)(2,1)} %bitcast.4), calls=%async_computation.2 | async-start | bytes 131072 | tf_op jit(solution)/shard_map/all_to_all | solution.py:486
  42.4 5.9 %copy-start.3 = (bf16[256,256]{1,0:T(8,128)(2,1)S(1)}, bf16[256,256]{1,0:T(8,128)(2,1)}, u32[]{:S(2)}) copy-start(bf16[256,256]{1,0:T(8,128)(2,1)} %out_w_ref.1) | copy-start | bytes 393220

commit v4 on v3

--- a/solution.py
+++ b/solution.py
@@ -16,10 +16,20 @@
 HEADS = 16
 HEAD_DIM = 16
 STATE = 128
+ROW_ORDER = (5, 7, 3, 1, 4, 6, 2, 0)
+COL_ORDER = (15, 14, 13, 12, 11, 10, 9, 8, 7, 6, 5, 4, 3, 2, 1, 0)
+ROW_PLACE = tuple(ROW_ORDER.index(i) for i in range(ROWS))
+MID_ORDER = (15, 14, 13, 12, 11, 10, 9, 8, 7, 6, 5, 4, 3, 2, 1, 0)
+MID_PLACE = tuple(MID_ORDER.index(i) for i in range(COLS))
+COL_PLACE = tuple(COL_ORDER.index(i) for i in range(COLS))
 
 
 def iota(shape, dim):
     return lax.broadcasted_iota(jnp.int32, shape, dim)
+
+
+def place_of(row):
+    return sum(jnp.where(row == i, ROW_PLACE[i], 0) for i in range(ROWS))
 
 
 def halves(x):
@@ -108,15 +118,15 @@
 
 def pack_col_kernel(got_ref, own_ref, meta_ref, out_ref, left_ref, right_ref):
     r = lax.axis_index("row")
-    up = got_ref[jnp.maximum(r - 1, 0)].astype(F32)[TR - 1 : TR, :]
-    down = got_ref[jnp.minimum(r + 1, ROWS - 1)].astype(F32)[0:1, :]
+    up = got_ref[place_of(jnp.maximum(r - 1, 0))].astype(F32)[TR - 1 : TR, :]
+    down = got_ref[place_of(jnp.minimum(r + 1, ROWS - 1))].astype(F32)[0:1, :]
     above = jnp.concatenate([up[:, j * D : (j + 1) * D] for j in range(TC)], axis=0)
     below = jnp.concatenate([down[:, j * D : (j + 1) * D] for j in range(TC)], axis=0)
     own = own_ref[...].astype(F32)
     extra = got_ref[:, :, TC * D :].astype(F32)
     logs = jnp.concatenate(
         [
-            jnp.concatenate([extra[s, 8 + half : 9 + half, :] for s in range(ROWS)], axis=0)
+            jnp.concatenate([extra[s, 8 + half : 9 + half, :] for s in ROW_PLACE], axis=0)
             for half in range(2)
         ],
         axis=1,
@@ -124,13 +134,14 @@
     rows = [above] + [own[i] for i in range(TR)] + [below]
     rows = [x.astype(BF16) for x in rows]
     logs = logs.astype(BF16)
-    for dest in range(COLS):
+    for dest, place in enumerate(MID_PLACE):
         for slot in range(3):
-            out_ref[dest, :, slot * D : (slot + 1) * D] = rows[dest + slot]
-        out_ref[dest, :, 3 * D : 4 * D] = logs
-        out_ref[dest, :, 4 * D :] = meta_ref[dest]
-    left_ref[...] = got_ref[:, :, 0:D]
-    right_ref[...] = got_ref[:, :, (TC - 1) * D : TC * D]
+            out_ref[place, :, slot * D : (slot + 1) * D] = rows[dest + slot]
+        out_ref[place, :, 3 * D : 4 * D] = logs
+        out_ref[place, :, 4 * D :] = meta_ref[dest]
+    for i, s in enumerate(ROW_PLACE):
+        left_ref[i] = got_ref[s, :, 0:D]
+        right_ref[i] = got_ref[s, :, (TC - 1) * D : TC * D]
 
 
 def normalised(hidden, gain):
@@ -210,7 +221,13 @@
 ):
     r = lax.axis_index("row")
     c = lax.axis_index("col")
-    logs = cols_ref[:, :, 3 * D : 4 * D].astype(F32).reshape(LINE, D).astype(BF16)
+    logs, *cells = [
+        jnp.stack([cols_ref[p, :, s * D : (s + 1) * D] for p in MID_PLACE])
+        .astype(F32)
+        .reshape(LINE, D)
+        for s in (3, 0, 1, 2)
+    ]
+    logs = logs.astype(BF16)
     tokens = silu(jnp.dot(logs, cond_ref[...], preferred_element_type=F32)).astype(BF16)
     meta = jnp.sum(cols_ref[:, :, 4 * D :].astype(F32), axis=0)
     trace = jnp.broadcast_to(meta[0:1, :], (8, LINE)).T[:, 0:1].astype(jnp.int32)
@@ -220,10 +237,7 @@
     tokens = jnp.dot(chosen, tokens, preferred_element_type=F32)
     tokens_ref[...] = tokens
     row = r * TR + c
-    cells = [
-        cols_ref[:, :, s * D : (s + 1) * D].astype(F32).reshape(LINE, D) for s in range(3)
-    ]
-    out_ref[...] = line_scan(
+    scanned = line_scan(
         cells,
         [tokens, tokens, tokens],
         [row > 0, True, row < LINE - 1],
@@ -237,6 +251,9 @@
         meta[1:2, :] + meta[2:3, :],
         w_ref,
         x_ref,
+    )
+    out_ref[...] = jnp.concatenate(
+        [scanned[i * TC : (i + 1) * TC, :] for i in COL_ORDER], axis=0
     ).astype(BF16)
 
 
@@ -276,7 +293,7 @@
         elif q == TC + 1:
             cells = right_ref[...]
         else:
-            cells = rows_ref[:, :, (q - 1) * D : q * D]
+            cells = jnp.stack([rows_ref[s, :, (q - 1) * D : q * D] for s in ROW_PLACE])
         line = jnp.clip(c * TC + q - 1, 0, LINE - 1)
         cells = cells.astype(F32).reshape(LINE, D) + tokens_ref[pl.ds(line, 1), :]
         normed_ref[q * LINE : (q + 1) * LINE, :] = normalised(cells, gain)
@@ -323,9 +340,9 @@
     owner = iota((TC, LINE), 1) >> 4
     high = jnp.zeros((TC, LINE), F32)
     low = jnp.zeros((TC, LINE), F32)
-    for s in range(ROWS):
-        high = jnp.where(owner == s, extra[s, :TC, :], high)
-        low = jnp.where(owner == (s + ROWS // 2) % ROWS, extra[s, :TC, :], low)
+    for i, s in enumerate(ROW_PLACE):
+        high = jnp.where(owner == i, extra[s, :TC, :], high)
+        low = jnp.where(owner == (i + ROWS // 2) % ROWS, extra[s, :TC, :], low)
     horizon = high + pltpu.roll(low, LINE // 2, 1)
     steps = []
     sums = []
@@ -389,7 +406,8 @@
 
 
 def finish_kernel(row_ref, col_ref, hidden_ref, gate_ref, wide_ref, out_w_ref, out_ref):
-    total = row_ref[...].astype(F32).reshape(LINE, D) + col_ref[...]
+    by_row = jnp.concatenate([row_ref[s].astype(F32) for s in COL_PLACE], axis=0)
+    total = by_row + col_ref[...]
     scale = lax.rsqrt(jnp.mean(total * total, axis=-1, keepdims=True) + 1e-05)
     gated = (total * scale * wide_ref[10:11, :] * gate_ref[...]).astype(BF16)
     branch = jnp.dot(gated, out_w_ref[...], preferred_element_type=F32)
@@ -456,7 +474,9 @@
         smem=1,
         pinned=(),
     )
-    from_rows = lax.all_to_all(packed, "row", 0, 0, tiled=True)
+    from_rows = lax.all_to_all(
+        packed, "row", 0, 0, tiled=True, axis_index_groups=[list(ROW_ORDER)]
+    )
     packed, first, last = call(
         pack_col_kernel,
         [((COLS, 8, 4 * D + LINE), BF16), ((ROWS, TR, D), BF16), ((ROWS, TR, D), BF16)],
@@ -467,7 +487,9 @@
     ends = COLS - 1
     right = lax.ppermute(first, "col", [(i + 1, i) for i in range(ends)])
     left = lax.ppermute(last, "col", [(i, i + 1) for i in range(ends)])
-    from_cols = lax.all_to_all(packed, "col", 0, 0, tiled=True)
+    from_cols = lax.all_to_all(
+        packed, "col", 0, 0, tiled=True, axis_index_groups=[list(MID_ORDER)]
+    )
     by_row, tokens = call(
         row_kernel,
         [((LINE, D), BF16), ((LINE, D), F32)],
@@ -483,7 +505,9 @@
             pltpu.VMEM((HEADS * LINE, D), BF16),
         ],
     )
-    by_row = lax.all_to_all(by_row.reshape(COLS, TC, D), "col", 0, 0, tiled=True)
+    by_row = lax.all_to_all(
+        by_row.reshape(COLS, TC, D), "col", 0, 0, tiled=True, axis_index_groups=[list(COL_ORDER)]
+    )
     hidden, gate, by_column = call(
         column_kernel,
         [((LINE, D), F32), ((LINE, D), F32), ((LINE, D), F32)],

time: 49.5 us -> 45.1 us (0.911)
  waiting for transfers between devices: 3.79 us -> 0.83 us
  blocking collectives: 18.1 us -> 15.8 us
  starting transfers between devices: 17.6 us -> 18.4 us
    all_to_all x2, waiting for transfers between devices: 3.79 us -> 0.83 us  [the longest x1 0.83 us: per_device(): lax.all_to_all(packed, 'col', 0, 0, tiled=True, axis_index_groups=[list(M...]
    all_to_all x1, blocking collectives: 18.1 us -> 15.8 us  [per_device(): lax.all_to_all(packed, 'row', 0, 0, tiled=True, axis_index_groups=[list(R...]
    all_to_all x2, starting transfers between devices: 12.2 us -> 14 us  [the longest x1 7.3 us: per_device(): lax.all_to_all(packed, 'col', 0, 0, tiled=True, axis_index_groups=[list(M...]
    ppermute x1, starting transfers between devices: 3.53 us -> 2.48 us  [per_device(): left = lax.ppermute(last, 'col', [(i, i + 1) for i in range(ends)])]
  transfers between devices with their start and end apart: 4 -> 4, of which waited for: 2 -> 1; matrix products, arithmetic and copies ran while one was open for 0% -> 0% of each run, Pallas kernels for 14% -> 15%
where the time goes in v4:
time: 45.1 us; the launch traced here: 44.7 us
  starting transfers between devices  18.4 us (41%)
  blocking collectives  15.8 us (35%)
  Pallas kernels  9.51 us (21%)
  waiting for transfers between devices  0.83 us (2%)
    all_to_all x1, blocking collectives, per_device(): lax.all_to_all(packed, 'row', 0, 0, tiled=True, axis_index_groups=[list(R...  15.8 us
    pallas_call x5, Pallas kernels, call(): pl.pallas_call(kernel, out_shape=[shape(s, d) for s, d in outs], in_specs...  9.51 us
    all_to_all x1, starting transfers between devices, per_device(): lax.all_to_all(packed, 'col', 0, 0, tiled=True, axis_index_groups=[list(M...  7.3 us
    all_to_all x1, starting transfers between devices, per_device(): lax.all_to_all(by_row.reshape(COLS, TC, D), 'col', 0, 0, tiled=True, axis...  6.7 us
    ppermute x1, starting transfers between devices, per_device(): left = lax.ppermute(last, 'col', [(i, i + 1) for i in range(ends)])  2.48 us
    ppermute x1, starting transfers between devices, per_device(): right = lax.ppermute(first, 'col', [(i + 1, i) for i in range(ends)])  1.92 us
  transfers between devices with their start and end apart: 4, of which 1 were waited for; matrix products, arithmetic and copies ran while one was open for 0% of the time, Pallas kernels for 15%

profile of v4, /device:TPU:1, one launch (start us, length us, event | category | flops | bytes accessed | tf_op | source)
XLA Modules:
  0.0 44.7 jit_solution(1202294150678465127)
XLA Ops:
  0.0 1.1 %pack_row_kernel.1 = (bf16[8,16,2176]{2,1,0:T(8,128)(2,1)S(1)}, bf16[16,8,128]{2,1,0:T(8,128)(2,1)S(1)}, bf16[16,8,256]{2,1,0:T(8,128)(2,1)S(1)}, f32[16,256]{1,0:T(8,128)S(1)}, f32[2,64,128]{2,1,0:T(8,128)S(1)}) custom-call(s32[8]{0:T(128)} %trace_ref.1, bf16[16,8,256]{2,1,0:T(8,128)(2,1)} %latent_ref.1, bf16[1,256]{1,0:T(2,128)(2,1)} %logs_ref.1, ...), custom_call_target="tpu_custom_call" | custom-call | tf_op jit(solution)/shard_map/pack_row_kernel/pallas_call | solution.py:427
  1.1 15.8 %all_to_all.15.got_ref.rows_ref = bf16[8,16,2176]{2,1,0:T(8,128)(2,1)S(1)} all-to-all(bf16[8,16,2176]{2,1,0:T(8,128)(2,1)S(1)} %get-tuple-element.18), channel_id=1, replica_groups={{80,112,48,16,64,96,32,0},{81,113,49,17,65,97,33,1},{82,114,50,18,66,98..., dimensions={0} | all-to-all | bytes 1114112 | tf_op jit(solution)/shard_map/all_to_all | solution.py:477
  17.0 0.0 copy-start
  17.0 0.8 %pack_col_kernel.1 = (bf16[16,8,1152]{2,1,0:T(8,128)(2,1)}, bf16[8,16,256]{2,1,0:T(8,128)(2,1)S(1)}, bf16[8,16,256]{2,1,0:T(8,128)(2,1)S(1)}) custom-call(bf16[8,16,2176]{2,1,0:T(8,128)(2,1)S(1)} %all_to_all.15.got_ref.rows_ref, bf16[16,8,256]{2,1,0:T(8,128)(2,1)S(1)} %get-tuple-element.19.own_ref, bf16[16,8,128]{2,1,0:T(8,128)(2,1)S(1)} %get-tuple-element.20.meta_ref), custom_call_target="tpu_custom_call" | custom-call | tf_op jit(solution)/shard_map/pack_col_kernel/pallas_call | solution.py:427
  17.7 0.0 copy-start.1
  17.7 0.0 copy-start.2
  17.7 0.0 copy-start.4
  17.7 7.3 %all-to-all-start.1 = ((bf16[16,8,1152]{2,1,0:T(8,128)(2,1)}), bf16[16,8,1152]{2,1,0:T(8,128)(2,1)S(1)}, u32[]{:S(2)}, u32[]{:S(2)}) async-start(bf16[16,8,1152]{2,1,0:T(8,128)(2,1)} %get-tuple-element.21), calls=%async_computation.1 | async-start | bytes 589824 | tf_op jit(solution)/shard_map/all_to_all | solution.py:490
  25.0 2.5 %collective-permute-start = (bf16[8,16,256]{2,1,0:T(8,128)(2,1)S(1)}, bf16[8,16,256]{2,1,0:T(8,128)(2,1)S(1)}, u32[]{:S(2)}, u32[]{:S(2)}) collective-permute-start(bf16[8,16,256]{2,1,0:T(8,128)(2,1)S(1)} %get-tuple-element.25), channel_id=1, source_target_pairs={{0,1},{1,2},{2,3},{3,4},{4,5},{5,6},{6,7},{7,8},{8,9},{9,10},{10,1... | collective-permute-start | bytes 196616 | tf_op jit(solution)/shard_map/ppermute | solution.py:489
  27.5 1.9 %collective-permute-start.1 = (bf16[8,16,256]{2,1,0:T(8,128)(2,1)S(1)}, bf16[8,16,256]{2,1,0:T(8,128)(2,1)S(1)}, u32[]{:S(2)}, u32[]{:S(2)}) collective-permute-start(bf16[8,16,256]{2,1,0:T(8,128)(2,1)S(1)} %get-tuple-element.26), channel_id=1, source_target_pairs={{1,0},{2,1},{3,2},{4,3},{5,4},{6,5},{7,6},{8,7},{9,8},{10,9},{11,1... | collective-permute-start | bytes 196616 | tf_op jit(solution)/shard_map/ppermute | solution.py:488
  29.4 0.8 %all-to-all-done.1.cols_ref = bf16[16,8,1152]{2,1,0:T(8,128)(2,1)S(1)} async-done(((bf16[16,8,1152]{2,1,0:T(8,128)(2,1)}), bf16[16,8,1152]{2,1,0:T(8,128)(2,1)S(1)}, u32[]{:S(2)}, u32[]{:S(2)}) %all-to-all-start.1) | async-done | bytes 294944 | tf_op jit(solution)/shard_map/all_to_all | solution.py:490
  30.3 0.0 copy-done
  30.3 0.0 copy-done.1
  30.3 0.0 copy-done.2
  30.3 0.0 copy-done.4
  30.3 2.8 %row_kernel.1 = (bf16[128,256]{1,0:T(8,128)(2,1)}, f32[128,256]{1,0:T(8,128)S(1)}) custom-call(bf16[16,8,1152]{2,1,0:T(8,128)(2,1)S(1)} %all-to-all-done.1.cols_ref, f32[16,256]{1,0:T(8,128)S(1)} %get-tuple-element.22.wide_ref, f32[2,64,128]{2,1,0:T(8,128)S(1)} %get-tuple-element.23.side_ref, bf16[256,256]{1,0:T(8,128)(2,1)S(1)} %copy-done.4, ...), custom_call_target="tpu_custom_call" | custom-call | tf_op jit(solution)/shard_map/row_kernel/pallas_call | solution.py:427
  33.1 6.7 %all-to-all-start.2 = ((bf16[16,8,256]{2,1,0:T(8,128)(2,1)}), bf16[16,8,256]{2,1,0:T(8,128)(2,1)S(1)}, u32[]{:S(2)}, u32[]{:S(2)}) async-start(bf16[16,8,256]{2,1,0:T(8,128)(2,1)} %bitcast.4), calls=%async_computation.2 | async-start | bytes 131072 | tf_op jit(solution)/shard_map/all_to_all | solution.py:508
  39.8 0.0 collective-permute-done.left_ref
  39.8 0.0 collective-permute-done.1.right_ref
  39.8 0.0 copy-start.3
  39.8 4.0 %column_kernel.1 = (f32[128,256]{1,0:T(8,128)S(1)}, f32[128,256]{1,0:T(8,128)S(1)}, f32[128,256]{1,0:T(8,128)S(1)}) custom-call(bf16[8,16,2176]{2,1,0:T(8,128)(2,1)S(1)} %all_to_all.15.got_ref.rows_ref, bf16[8,16,256]{2,1,0:T(8,128)(2,1)S(1)} %collective-permute-done.left_ref, bf16[8,16,256]{2,1,0:T(8,128)(2,1)S(1)} %collective-permute-done.1.right_ref, ...), custom_call_target="tpu_custom_call" | custom-call | tf_op jit(solution)/shard_map/column_kernel/pallas_call | solution.py:427
  43.8 0.0 all-to-all-done.2.row_ref
  43.8 0.0 copy-done.3
  43.8 0.9 %finish_kernel.1 = bf16[16,8,256]{2,1,0:T(8,128)(2,1)} custom-call(bf16[16,8,256]{2,1,0:T(8,128)(2,1)S(1)} %all-to-all-done.2.row_ref, f32[128,256]{1,0:T(8,128)S(1)} %get-tuple-element.28.col_ref, f32[128,256]{1,0:T(8,128)S(1)} %get-tuple-element.29.hidden_ref, f32[128,256]{1,0:T(8,128)S(1)} %get-tuple-element.30.gate_ref, ...), custom_call_target="tpu_custom_call" | custom-call | tf_op jit(solution)/shard_map/finish_kernel/pallas_call | solution.py:427
Async XLA Ops:
  17.0 13.3 %copy-start = (bf16[256,1024]{1,0:T(8,128)(2,1)S(1)}, bf16[256,1024]{1,0:T(8,128)(2,1)}, u32[]{:S(2)}) copy-start(bf16[256,1024]{1,0:T(8,128)(2,1)} %bc_ref.3) | copy-start | bytes 1572868
  17.7 12.6 %copy-start.1 = (bf16[256,512]{1,0:T(8,128)(2,1)S(1)}, bf16[256,512]{1,0:T(8,128)(2,1)}, u32[]{:S(2)}) copy-start(bf16[256,512]{1,0:T(8,128)(2,1)} %in_ref.3) | copy-start | bytes 786436
  17.7 12.6 %copy-start.2 = (bf16[256,64]{0,1:T(8,128)(2,1)S(1)}, bf16[256,64]{0,1:T(8,128)(2,1)}, u32[]{:S(2)}) copy-start(bf16[256,64]{0,1:T(8,128)(2,1)} %param.23) | copy-start | bytes 98308
  17.7 12.6 %copy-start.4 = (bf16[256,256]{1,0:T(8,128)(2,1)S(1)}, bf16[256,256]{1,0:T(8,128)(2,1)}, u32[]{:S(2)}) copy-start(bf16[256,256]{1,0:T(8,128)(2,1)} %cond_ref.1) | copy-start | bytes 393220
  17.7 12.5 %all-to-all-start.1 = ((bf16[16,8,1152]{2,1,0:T(8,128)(2,1)}), bf16[16,8,1152]{2,1,0:T(8,128)(2,1)S(1)}, u32[]{:S(2)}, u32[]{:S(2)}) async-start(bf16[16,8,1152]{2,1,0:T(8,128)(2,1)} %get-tuple-element.21), calls=%async_computation.1 | async-start | bytes 589824 | tf_op jit(solution)/shard_map/all_to_all | solution.py:490
  25.0 14.7 %collective-permute-start = (bf16[8,16,256]{2,1,0:T(8,128)(2,1)S(1)}, bf16[8,16,256]{2,1,0:T(8,128)(2,1)S(1)}, u32[]{:S(2)}, u32[]{:S(2)}) collective-permute-start(bf16[8,16,256]{2,1,0:T(8,128)(2,1)S(1)} %get-tuple-element.25), channel_id=1, source_target_pairs={{0,1},{1,2},{2,3},{3,4},{4,5},{5,6},{6,7},{7,8},{8,9},{9,10},{10,1... | collective-permute-start | bytes 196616 | tf_op jit(solution)/shard_map/ppermute | solution.py:489
  27.5 12.3 %collective-permute-start.1 = (bf16[8,16,256]{2,1,0:T(8,128)(2,1)S(1)}, bf16[8,16,256]{2,1,0:T(8,128)(2,1)S(1)}, u32[]{:S(2)}, u32[]{:S(2)}) collective-permute-start(bf16[8,16,256]{2,1,0:T(8,128)(2,1)S(1)} %get-tuple-element.26), channel_id=1, source_target_pairs={{1,0},{2,1},{3,2},{4,3},{5,4},{6,5},{7,6},{8,7},{9,8},{10,9},{11,1... | collective-permute-start | bytes 196616 | tf_op jit(solution)/shard_map/ppermute | solution.py:488
  33.1 10.7 %all-to-all-start.2 = ((bf16[16,8,256]{2,1,0:T(8,128)(2,1)}), bf16[16,8,256]{2,1,0:T(8,128)(2,1)S(1)}, u32[]{:S(2)}, u32[]{:S(2)}) async-start(bf16[16,8,256]{2,1,0:T(8,128)(2,1)} %bitcast.4), calls=%async_computation.2 | async-start | bytes 131072 | tf_op jit(solution)/shard_map/all_to_all | solution.py:508
  39.8 4.0 %copy-start.3 = (bf16[256,256]{1,0:T(8,128)(2,1)S(1)}, bf16[256,256]{1,0:T(8,128)(2,1)}, u32[]{:S(2)}) copy-start(bf16[256,256]{1,0:T(8,128)(2,1)} %out_w_ref.1) | copy-start | bytes 393220

commit v5 on v4

--- a/solution.py
+++ b/solution.py
@@ -329,7 +329,10 @@
     mine = jnp.concatenate(
         [mixed_ref[pl.ds(j * LINE + start, TR), :] for j in range(TC)], axis=0
     )
-    c_own = jnp.dot(mine, c_weight, preferred_element_type=F32).astype(BF16)
+    c_own = jnp.dot(mine, c_weight, preferred_element_type=F32)
+    ahead_lane = iota((LINE, D), 1) < STATE
+    c_ahead = jnp.where(ahead_lane, c_own, 0.0).astype(BF16)
+    c_behind = jnp.where(ahead_lane, 0.0, c_own).astype(BF16)
     contract = (((1,), (1,)), ((), ()))
     z = lax.dot_general(
         dt_ref[2 * HEADS :, :], mixed_ref[...], contract, preferred_element_type=F32
@@ -372,18 +375,17 @@
     other = iota((TR, LINE), 1)
     lower = other <= at
     upper = other >= at
-    head_of = iota((TR, D), 1) // HEAD_DIM
+    head_of = iota((TR, LINE), 1) >> 4
     for j in range(TC):
-        cj = c_own[j * TR : (j + 1) * TR, :]
-        bj = b_ref[j * LINE : (j + 1) * LINE, :]
-        score_f = lax.dot_general(
-            cj[:, :STATE], bj[:, :STATE], contract, preferred_element_type=F32
+        at = slice(j * TR, (j + 1) * TR)
+        scores = lax.dot_general(
+            jnp.concatenate([c_ahead[at], c_behind[at]], axis=0),
+            b_ref[j * LINE : (j + 1) * LINE, :],
+            contract,
+            preferred_element_type=F32,
         )
-        score_b = lax.dot_general(
-            cj[:, STATE:], bj[:, STATE:], contract, preferred_element_type=F32
-        )
-        score_f = jnp.where(lower, score_f, 0.0)
-        score_b = jnp.where(upper, score_b, 0.0)
+        score_f = jnp.where(lower, scores[:TR], 0.0)
+        score_b = jnp.where(upper, scores[TR:], 0.0)
         for h in range(HEADS):
             n = j * HEADS + h
             ahead = ahead_own[:, n : n + 1] - sums[0][n : n + 1, :]
@@ -391,13 +393,17 @@
             decay = jnp.exp(jnp.where(lower, ahead, behind))
             drive = score_f * steps[0][j][h : h + 1, :] + score_b * steps[1][j][h : h + 1, :]
             w_ref[j, h * TR : (h + 1) * TR, :] = (drive * decay).astype(BF16)
-        full = jnp.dot(
-            w_ref[j], mixed_ref[j * LINE : (j + 1) * LINE, :], preferred_element_type=F32
-        )
-        got = full[:TR, :]
-        for h in range(1, HEADS):
-            got = jnp.where(head_of == h, full[h * TR : (h + 1) * TR, :], got)
-        y_ref[j * TR : (j + 1) * TR, :] = got
+        for half in range(2):
+            at = slice(half * LINE, (half + 1) * LINE)
+            full = jnp.dot(
+                w_ref[j, at, :],
+                mixed_ref[j * LINE : (j + 1) * LINE, at],
+                preferred_element_type=F32,
+            )
+            got = full[:TR, :]
+            for h in range(1, HEADS // 2):
+                got = jnp.where(head_of == h, full[h * TR : (h + 1) * TR, :], got)
+            y_ref[j * TR : (j + 1) * TR, at] = got
     pick = ((k % TC) * TR + k // TC == j_).astype(BF16)
     high, low = halves(y_ref[...])
     sum_ref[...] = jnp.dot(pick, high.astype(BF16), preferred_element_type=F32) + jnp.dot(

time: 45.1 us -> 44.5 us (0.987)
  Pallas kernels: 9.51 us -> 8.95 us
    pallas_call x5, Pallas kernels: 9.51 us -> 8.95 us  [call(): pl.pallas_call(kernel, out_shape=[shape(s, d) for s, d in outs], in_specs...]
  transfers between devices with their start and end apart: 4 -> 4, of which waited for: 1 -> 1; matrix products, arithmetic and copies ran while one was open for 0% -> 0% of each run, Pallas kernels for 15% -> 14%
where the time goes in v5:
time: 44.5 us; the launch traced here: 44.1 us
  starting transfers between devices  18.4 us (41%)
  blocking collectives  15.8 us (36%)
  Pallas kernels  8.95 us (20%)
  waiting for transfers between devices  0.83 us (2%)
    all_to_all x1, blocking collectives, per_device(): lax.all_to_all(packed, 'row', 0, 0, tiled=True, axis_index_groups=[list(R...  15.8 us
    pallas_call x5, Pallas kernels, call(): pl.pallas_call(kernel, out_shape=[shape(s, d) for s, d in outs], in_specs...  8.95 us
    all_to_all x1, starting transfers between devices, per_device(): lax.all_to_all(packed, 'col', 0, 0, tiled=True, axis_index_groups=[list(M...  7.3 us
    all_to_all x1, starting transfers between devices, per_device(): lax.all_to_all(by_row.reshape(COLS, TC, D), 'col', 0, 0, tiled=True, axis...  6.7 us
    ppermute x1, starting transfers between devices, per_device(): left = lax.ppermute(last, 'col', [(i, i + 1) for i in range(ends)])  2.48 us
    ppermute x1, starting transfers between devices, per_device(): right = lax.ppermute(first, 'col', [(i + 1, i) for i in range(ends)])  1.92 us
  transfers between devices with their start and end apart: 4, of which 1 were waited for; matrix products, arithmetic and copies ran while one was open for 0% of the time, Pallas kernels for 14%

profile of v5, /device:TPU:1, one launch (start us, length us, event | category | flops | bytes accessed | tf_op | source)
XLA Modules:
  0.0 44.1 jit_solution(2068605268044193165)
XLA Ops:
  0.0 1.1 %pack_row_kernel.1 = (bf16[8,16,2176]{2,1,0:T(8,128)(2,1)S(1)}, bf16[16,8,128]{2,1,0:T(8,128)(2,1)S(1)}, bf16[16,8,256]{2,1,0:T(8,128)(2,1)S(1)}, f32[16,256]{1,0:T(8,128)S(1)}, f32[2,64,128]{2,1,0:T(8,128)S(1)}) custom-call(s32[8]{0:T(128)} %trace_ref.1, bf16[16,8,256]{2,1,0:T(8,128)(2,1)} %latent_ref.1, bf16[1,256]{1,0:T(2,128)(2,1)} %logs_ref.1, ...), custom_call_target="tpu_custom_call" | custom-call | tf_op jit(solution)/shard_map/pack_row_kernel/pallas_call | solution.py:433
  1.1 15.8 %all_to_all.15.got_ref.rows_ref = bf16[8,16,2176]{2,1,0:T(8,128)(2,1)S(1)} all-to-all(bf16[8,16,2176]{2,1,0:T(8,128)(2,1)S(1)} %get-tuple-element.18), channel_id=1, replica_groups={{80,112,48,16,64,96,32,0},{81,113,49,17,65,97,33,1},{82,114,50,18,66,98..., dimensions={0} | all-to-all | bytes 1114112 | tf_op jit(solution)/shard_map/all_to_all | solution.py:483
  17.0 0.0 copy-start
  17.0 0.8 %pack_col_kernel.1 = (bf16[16,8,1152]{2,1,0:T(8,128)(2,1)}, bf16[8,16,256]{2,1,0:T(8,128)(2,1)S(1)}, bf16[8,16,256]{2,1,0:T(8,128)(2,1)S(1)}) custom-call(bf16[8,16,2176]{2,1,0:T(8,128)(2,1)S(1)} %all_to_all.15.got_ref.rows_ref, bf16[16,8,256]{2,1,0:T(8,128)(2,1)S(1)} %get-tuple-element.19.own_ref, bf16[16,8,128]{2,1,0:T(8,128)(2,1)S(1)} %get-tuple-element.20.meta_ref), custom_call_target="tpu_custom_call" | custom-call | tf_op jit(solution)/shard_map/pack_col_kernel/pallas_call | solution.py:433
  17.7 0.0 copy-start.1
  17.7 0.0 copy-start.2
  17.7 0.0 copy-start.4
  17.7 7.3 %all-to-all-start.1 = ((bf16[16,8,1152]{2,1,0:T(8,128)(2,1)}), bf16[16,8,1152]{2,1,0:T(8,128)(2,1)S(1)}, u32[]{:S(2)}, u32[]{:S(2)}) async-start(bf16[16,8,1152]{2,1,0:T(8,128)(2,1)} %get-tuple-element.21), calls=%async_computation.1 | async-start | bytes 589824 | tf_op jit(solution)/shard_map/all_to_all | solution.py:496
  25.0 2.5 %collective-permute-start = (bf16[8,16,256]{2,1,0:T(8,128)(2,1)S(1)}, bf16[8,16,256]{2,1,0:T(8,128)(2,1)S(1)}, u32[]{:S(2)}, u32[]{:S(2)}) collective-permute-start(bf16[8,16,256]{2,1,0:T(8,128)(2,1)S(1)} %get-tuple-element.25), channel_id=1, source_target_pairs={{0,1},{1,2},{2,3},{3,4},{4,5},{5,6},{6,7},{7,8},{8,9},{9,10},{10,1... | collective-permute-start | bytes 196616 | tf_op jit(solution)/shard_map/ppermute | solution.py:495
  27.5 1.9 %collective-permute-start.1 = (bf16[8,16,256]{2,1,0:T(8,128)(2,1)S(1)}, bf16[8,16,256]{2,1,0:T(8,128)(2,1)S(1)}, u32[]{:S(2)}, u32[]{:S(2)}) collective-permute-start(bf16[8,16,256]{2,1,0:T(8,128)(2,1)S(1)} %get-tuple-element.26), channel_id=1, source_target_pairs={{1,0},{2,1},{3,2},{4,3},{5,4},{6,5},{7,6},{8,7},{9,8},{10,9},{11,1... | collective-permute-start | bytes 196616 | tf_op jit(solution)/shard_map/ppermute | solution.py:494
  29.4 0.8 %all-to-all-done.1.cols_ref = bf16[16,8,1152]{2,1,0:T(8,128)(2,1)S(1)} async-done(((bf16[16,8,1152]{2,1,0:T(8,128)(2,1)}), bf16[16,8,1152]{2,1,0:T(8,128)(2,1)S(1)}, u32[]{:S(2)}, u32[]{:S(2)}) %all-to-all-start.1) | async-done | bytes 294944 | tf_op jit(solution)/shard_map/all_to_all | solution.py:496
  30.3 0.0 copy-done
  30.3 0.0 copy-done.1
  30.3 0.0 copy-done.2
  30.3 0.0 copy-done.4
  30.3 2.8 %row_kernel.1 = (bf16[128,256]{1,0:T(8,128)(2,1)}, f32[128,256]{1,0:T(8,128)S(1)}) custom-call(bf16[16,8,1152]{2,1,0:T(8,128)(2,1)S(1)} %all-to-all-done.1.cols_ref, f32[16,256]{1,0:T(8,128)S(1)} %get-tuple-element.22.wide_ref, f32[2,64,128]{2,1,0:T(8,128)S(1)} %get-tuple-element.23.side_ref, bf16[256,256]{1,0:T(8,128)(2,1)S(1)} %copy-done.4, ...), custom_call_target="tpu_custom_call" | custom-call | tf_op jit(solution)/shard_map/row_kernel/pallas_call | solution.py:433
  33.1 6.7 %all-to-all-start.2 = ((bf16[16,8,256]{2,1,0:T(8,128)(2,1)}), bf16[16,8,256]{2,1,0:T(8,128)(2,1)S(1)}, u32[]{:S(2)}, u32[]{:S(2)}) async-start(bf16[16,8,256]{2,1,0:T(8,128)(2,1)} %bitcast.4), calls=%async_computation.2 | async-start | bytes 131072 | tf_op jit(solution)/shard_map/all_to_all | solution.py:514
  39.8 0.0 collective-permute-done.left_ref
  39.8 0.0 collective-permute-done.1.right_ref
  39.8 0.0 copy-start.3
  39.8 3.4 %column_kernel.1 = (f32[128,256]{1,0:T(8,128)S(1)}, f32[128,256]{1,0:T(8,128)S(1)}, f32[128,256]{1,0:T(8,128)S(1)}) custom-call(bf16[8,16,2176]{2,1,0:T(8,128)(2,1)S(1)} %all_to_all.15.got_ref.rows_ref, bf16[8,16,256]{2,1,0:T(8,128)(2,1)S(1)} %collective-permute-done.left_ref, bf16[8,16,256]{2,1,0:T(8,128)(2,1)S(1)} %collective-permute-done.1.right_ref, ...), custom_call_target="tpu_custom_call" | custom-call | tf_op jit(solution)/shard_map/column_kernel/pallas_call | solution.py:433
  43.2 0.0 all-to-all-done.2.row_ref
  43.2 0.0 copy-done.3
  43.2 0.9 %finish_kernel.1 = bf16[16,8,256]{2,1,0:T(8,128)(2,1)} custom-call(bf16[16,8,256]{2,1,0:T(8,128)(2,1)S(1)} %all-to-all-done.2.row_ref, f32[128,256]{1,0:T(8,128)S(1)} %get-tuple-element.28.col_ref, f32[128,256]{1,0:T(8,128)S(1)} %get-tuple-element.29.hidden_ref, f32[128,256]{1,0:T(8,128)S(1)} %get-tuple-element.30.gate_ref, ...), custom_call_target="tpu_custom_call" | custom-call | tf_op jit(solution)/shard_map/finish_kernel/pallas_call | solution.py:433
Async XLA Ops:
  17.0 13.3 %copy-start = (bf16[256,1024]{1,0:T(8,128)(2,1)S(1)}, bf16[256,1024]{1,0:T(8,128)(2,1)}, u32[]{:S(2)}) copy-start(bf16[256,1024]{1,0:T(8,128)(2,1)} %bc_ref.3) | copy-start | bytes 1572868
  17.7 12.6 %copy-start.1 = (bf16[256,512]{1,0:T(8,128)(2,1)S(1)}, bf16[256,512]{1,0:T(8,128)(2,1)}, u32[]{:S(2)}) copy-start(bf16[256,512]{1,0:T(8,128)(2,1)} %in_ref.3) | copy-start | bytes 786436
  17.7 12.6 %copy-start.2 = (bf16[256,64]{0,1:T(8,128)(2,1)S(1)}, bf16[256,64]{0,1:T(8,128)(2,1)}, u32[]{:S(2)}) copy-start(bf16[256,64]{0,1:T(8,128)(2,1)} %param.23) | copy-start | bytes 98308
  17.7 12.6 %copy-start.4 = (bf16[256,256]{1,0:T(8,128)(2,1)S(1)}, bf16[256,256]{1,0:T(8,128)(2,1)}, u32[]{:S(2)}) copy-start(bf16[256,256]{1,0:T(8,128)(2,1)} %cond_ref.1) | copy-start | bytes 393220
  17.7 12.5 %all-to-all-start.1 = ((bf16[16,8,1152]{2,1,0:T(8,128)(2,1)}), bf16[16,8,1152]{2,1,0:T(8,128)(2,1)S(1)}, u32[]{:S(2)}, u32[]{:S(2)}) async-start(bf16[16,8,1152]{2,1,0:T(8,128)(2,1)} %get-tuple-element.21), calls=%async_computation.1 | async-start | bytes 589824 | tf_op jit(solution)/shard_map/all_to_all | solution.py:496
  25.0 14.7 %collective-permute-start = (bf16[8,16,256]{2,1,0:T(8,128)(2,1)S(1)}, bf16[8,16,256]{2,1,0:T(8,128)(2,1)S(1)}, u32[]{:S(2)}, u32[]{:S(2)}) collective-permute-start(bf16[8,16,256]{2,1,0:T(8,128)(2,1)S(1)} %get-tuple-element.25), channel_id=1, source_target_pairs={{0,1},{1,2},{2,3},{3,4},{4,5},{5,6},{6,7},{7,8},{8,9},{9,10},{10,1... | collective-permute-start | bytes 196616 | tf_op jit(solution)/shard_map/ppermute | solution.py:495
  27.5 12.3 %collective-permute-start.1 = (bf16[8,16,256]{2,1,0:T(8,128)(2,1)S(1)}, bf16[8,16,256]{2,1,0:T(8,128)(2,1)S(1)}, u32[]{:S(2)}, u32[]{:S(2)}) collective-permute-start(bf16[8,16,256]{2,1,0:T(8,128)(2,1)S(1)} %get-tuple-element.26), channel_id=1, source_target_pairs={{1,0},{2,1},{3,2},{4,3},{5,4},{6,5},{7,6},{8,7},{9,8},{10,9},{11,1... | collective-permute-start | bytes 196616 | tf_op jit(solution)/shard_map/ppermute | solution.py:494
  33.1 10.2 %all-to-all-start.2 = ((bf16[16,8,256]{2,1,0:T(8,128)(2,1)}), bf16[16,8,256]{2,1,0:T(8,128)(2,1)S(1)}, u32[]{:S(2)}, u32[]{:S(2)}) async-start(bf16[16,8,256]{2,1,0:T(8,128)(2,1)} %bitcast.4), calls=%async_computation.2 | async-start | bytes 131072 | tf_op jit(solution)/shard_map/all_to_all | solution.py:514
  39.8 3.4 %copy-start.3 = (bf16[256,256]{1,0:T(8,128)(2,1)S(1)}, bf16[256,256]{1,0:T(8,128)(2,1)}, u32[]{:S(2)}) copy-start(bf16[256,256]{1,0:T(8,128)(2,1)} %out_w_ref.1) | copy-start | bytes 393220

commit v6 on v5

--- a/solution.py
+++ b/solution.py
@@ -116,8 +116,9 @@
         )
 
 
-def pack_col_kernel(got_ref, own_ref, meta_ref, out_ref, left_ref, right_ref):
+def pack_col_kernel(got_ref, own_ref, meta_ref, out_ref, near_ref, far_ref):
     r = lax.axis_index("row")
+    even = (lax.axis_index("col") & 1) == 0
     up = got_ref[place_of(jnp.maximum(r - 1, 0))].astype(F32)[TR - 1 : TR, :]
     down = got_ref[place_of(jnp.minimum(r + 1, ROWS - 1))].astype(F32)[0:1, :]
     above = jnp.concatenate([up[:, j * D : (j + 1) * D] for j in range(TC)], axis=0)
@@ -140,8 +141,10 @@
         out_ref[place, :, 3 * D : 4 * D] = logs
         out_ref[place, :, 4 * D :] = meta_ref[dest]
     for i, s in enumerate(ROW_PLACE):
-        left_ref[i] = got_ref[s, :, 0:D]
-        right_ref[i] = got_ref[s, :, (TC - 1) * D : TC * D]
+        first = got_ref[s, :, 0:D]
+        last = got_ref[s, :, (TC - 1) * D : TC * D]
+        near_ref[i] = jnp.where(even, last, first)
+        far_ref[i] = jnp.where(even, first, last)
 
 
 def normalised(hidden, gain):
@@ -259,8 +262,8 @@
 
 def column_kernel(
     rows_ref,
-    left_ref,
-    right_ref,
+    near_ref,
+    far_ref,
     tokens_ref,
     own_ref,
     wide_ref,
@@ -289,9 +292,9 @@
     gate_ref[...] = silu(gate.astype(BF16).astype(F32))
     for q in range(TC + 2):
         if q == 0:
-            cells = left_ref[...]
+            cells = jnp.where((c & 1) == 0, far_ref[...], near_ref[...])
         elif q == TC + 1:
-            cells = right_ref[...]
+            cells = jnp.where((c & 1) == 0, near_ref[...], far_ref[...])
         else:
             cells = jnp.stack([rows_ref[s, :, (q - 1) * D : q * D] for s in ROW_PLACE])
         line = jnp.clip(c * TC + q - 1, 0, LINE - 1)
@@ -483,16 +486,16 @@
     from_rows = lax.all_to_all(
         packed, "row", 0, 0, tiled=True, axis_index_groups=[list(ROW_ORDER)]
     )
-    packed, first, last = call(
+    packed, near, far = call(
         pack_col_kernel,
         [((COLS, 8, 4 * D + LINE), BF16), ((ROWS, TR, D), BF16), ((ROWS, TR, D), BF16)],
         from_rows,
         own,
         meta,
     )
-    ends = COLS - 1
-    right = lax.ppermute(first, "col", [(i + 1, i) for i in range(ends)])
-    left = lax.ppermute(last, "col", [(i, i + 1) for i in range(ends)])
+    near = lax.ppermute(near, "col", [(i, i ^ 1) for i in range(COLS)])
+    pairs = [(i, i + 1) for i in range(1, COLS - 1, 2)]
+    far = lax.ppermute(far, "col", pairs + [(j, i) for i, j in pairs])
     from_cols = lax.all_to_all(
         packed, "col", 0, 0, tiled=True, axis_index_groups=[list(MID_ORDER)]
     )
@@ -518,8 +521,8 @@
         column_kernel,
         [((LINE, D), F32), ((LINE, D), F32), ((LINE, D), F32)],
         from_rows,
-        left,
-        right,
+        near,
+        far,
         tokens,
         own,
         wide,

time: 44.5 us -> 43.4 us (0.975)
  starting transfers between devices: 18.4 us -> 15.5 us
  waiting for transfers between devices: 0.83 us -> 2.68 us
    all_to_all x1, waiting for transfers between devices: 0.83 us -> 2.67 us  [per_device(): lax.all_to_all(packed, 'col', 0, 0, tiled=True, axis_index_groups=[list(M...]
    ppermute x2, starting transfers between devices: 4.4 us -> 2.56 us  [the longest x1 2.13 us: per_device(): far = lax.ppermute(far, 'col', pairs + [(j, i) for i, j in pairs])]
    all_to_all x1, starting transfers between devices: 6.7 us -> 5.66 us  [per_device(): lax.all_to_all(by_row.reshape(COLS, TC, D), 'col', 0, 0, tiled=True, axis...]
where the time goes in v6:
time: 43.4 us; the launch traced here: 43.1 us
  blocking collectives  15.8 us (36%)
  starting transfers between devices  15.5 us (36%)
  Pallas kernels  8.96 us (21%)
  waiting for transfers between devices  2.68 us (6%)
    all_to_all x1, blocking collectives, per_device(): lax.all_to_all(packed, 'row', 0, 0, tiled=True, axis_index_groups=[list(R...  15.8 us
    pallas_call x5, Pallas kernels, call(): pl.pallas_call(kernel, out_shape=[shape(s, d) for s, d in outs], in_specs...  8.96 us
    all_to_all x1, starting transfers between devices, per_device(): lax.all_to_all(packed, 'col', 0, 0, tiled=True, axis_index_groups=[list(M...  7.3 us
    all_to_all x1, starting transfers between devices, per_device(): lax.all_to_all(by_row.reshape(COLS, TC, D), 'col', 0, 0, tiled=True, axis...  5.66 us
    all_to_all x1, waiting for transfers between devices, per_device(): lax.all_to_all(packed, 'col', 0, 0, tiled=True, axis_index_groups=[list(M...  2.67 us
    ppermute x1, starting transfers between devices, per_device(): far = lax.ppermute(far, 'col', pairs + [(j, i) for i, j in pairs])  2.13 us
  transfers between devices with their start and end apart: 4, of which 1 were waited for; matrix products, arithmetic and copies ran while one was open for 0% of the time, Pallas kernels for 14%

profile of v6, /device:TPU:1, one launch (start us, length us, event | category | flops | bytes accessed | tf_op | source)
XLA Modules:
  0.0 43.1 jit_solution(18290491046231318340)
XLA Ops:
  0.0 1.1 %pack_row_kernel.1 = (bf16[8,16,2176]{2,1,0:T(8,128)(2,1)S(1)}, bf16[16,8,128]{2,1,0:T(8,128)(2,1)S(1)}, bf16[16,8,256]{2,1,0:T(8,128)(2,1)S(1)}, f32[16,256]{1,0:T(8,128)S(1)}, f32[2,64,128]{2,1,0:T(8,128)S(1)}) custom-call(s32[8]{0:T(128)} %trace_ref.1, bf16[16,8,256]{2,1,0:T(8,128)(2,1)} %latent_ref.1, bf16[1,256]{1,0:T(2,128)(2,1)} %logs_ref.1, ...), custom_call_target="tpu_custom_call" | custom-call | tf_op jit(solution)/shard_map/pack_row_kernel/pallas_call | solution.py:436
  1.1 15.8 %all_to_all.15.got_ref.rows_ref = bf16[8,16,2176]{2,1,0:T(8,128)(2,1)S(1)} all-to-all(bf16[8,16,2176]{2,1,0:T(8,128)(2,1)S(1)} %get-tuple-element.18), channel_id=1, replica_groups={{80,112,48,16,64,96,32,0},{81,113,49,17,65,97,33,1},{82,114,50,18,66,98..., dimensions={0} | all-to-all | bytes 1114112 | tf_op jit(solution)/shard_map/all_to_all | solution.py:486
  17.0 0.0 copy-start
  17.0 0.8 %pack_col_kernel.1 = (bf16[16,8,1152]{2,1,0:T(8,128)(2,1)}, bf16[8,16,256]{2,1,0:T(8,128)(2,1)S(1)}, bf16[8,16,256]{2,1,0:T(8,128)(2,1)S(1)}) custom-call(bf16[8,16,2176]{2,1,0:T(8,128)(2,1)S(1)} %all_to_all.15.got_ref.rows_ref, bf16[16,8,256]{2,1,0:T(8,128)(2,1)S(1)} %get-tuple-element.19.own_ref, bf16[16,8,128]{2,1,0:T(8,128)(2,1)S(1)} %get-tuple-element.20.meta_ref), custom_call_target="tpu_custom_call" | custom-call | tf_op jit(solution)/shard_map/pack_col_kernel/pallas_call | solution.py:436
  17.7 0.0 copy-start.1
  17.7 0.0 copy-start.2
  17.7 0.0 copy-start.4
  17.7 7.3 %all-to-all-start.1 = ((bf16[16,8,1152]{2,1,0:T(8,128)(2,1)}), bf16[16,8,1152]{2,1,0:T(8,128)(2,1)S(1)}, u32[]{:S(2)}, u32[]{:S(2)}) async-start(bf16[16,8,1152]{2,1,0:T(8,128)(2,1)} %get-tuple-element.21), calls=%async_computation.1 | async-start | bytes 589824 | tf_op jit(solution)/shard_map/all_to_all | solution.py:499
  25.0 0.4 collective-permute-start
  25.5 2.1 %collective-permute-start.1 = (bf16[8,16,256]{2,1,0:T(8,128)(2,1)S(1)}, bf16[8,16,256]{2,1,0:T(8,128)(2,1)S(1)}, u32[]{:S(2)}, u32[]{:S(2)}) collective-permute-start(bf16[8,16,256]{2,1,0:T(8,128)(2,1)S(1)} %get-tuple-element.26), channel_id=1, source_target_pairs={{1,2},{3,4},{5,6},{7,8},{9,10},{11,12},{13,14},{2,1},{4,3},{6,5},{... | collective-permute-start | bytes 196616 | tf_op jit(solution)/shard_map/ppermute | solution.py:498
  27.6 2.7 %all-to-all-done.1.cols_ref = bf16[16,8,1152]{2,1,0:T(8,128)(2,1)S(1)} async-done(((bf16[16,8,1152]{2,1,0:T(8,128)(2,1)}), bf16[16,8,1152]{2,1,0:T(8,128)(2,1)S(1)}, u32[]{:S(2)}, u32[]{:S(2)}) %all-to-all-start.1) | async-done | bytes 294944 | tf_op jit(solution)/shard_map/all_to_all | solution.py:499
  30.3 0.0 copy-done
  30.3 0.0 copy-done.1
  30.3 0.0 copy-done.2
  30.3 0.0 copy-done.4
  30.3 2.8 %row_kernel.1 = (bf16[128,256]{1,0:T(8,128)(2,1)}, f32[128,256]{1,0:T(8,128)S(1)}) custom-call(bf16[16,8,1152]{2,1,0:T(8,128)(2,1)S(1)} %all-to-all-done.1.cols_ref, f32[16,256]{1,0:T(8,128)S(1)} %get-tuple-element.22.wide_ref, f32[2,64,128]{2,1,0:T(8,128)S(1)} %get-tuple-element.23.side_ref, bf16[256,256]{1,0:T(8,128)(2,1)S(1)} %copy-done.4, ...), custom_call_target="tpu_custom_call" | custom-call | tf_op jit(solution)/shard_map/row_kernel/pallas_call | solution.py:436
  33.1 5.7 %all-to-all-start.2 = ((bf16[16,8,256]{2,1,0:T(8,128)(2,1)}), bf16[16,8,256]{2,1,0:T(8,128)(2,1)S(1)}, u32[]{:S(2)}, u32[]{:S(2)}) async-start(bf16[16,8,256]{2,1,0:T(8,128)(2,1)} %bitcast.4), calls=%async_computation.2 | async-start | bytes 131072 | tf_op jit(solution)/shard_map/all_to_all | solution.py:517
  38.7 0.0 collective-permute-done.near_ref
  38.7 0.0 collective-permute-done.1.far_ref
  38.7 0.0 copy-start.3
  38.8 3.4 %column_kernel.1 = (f32[128,256]{1,0:T(8,128)S(1)}, f32[128,256]{1,0:T(8,128)S(1)}, f32[128,256]{1,0:T(8,128)S(1)}) custom-call(bf16[8,16,2176]{2,1,0:T(8,128)(2,1)S(1)} %all_to_all.15.got_ref.rows_ref, bf16[8,16,256]{2,1,0:T(8,128)(2,1)S(1)} %collective-permute-done.near_ref, bf16[8,16,256]{2,1,0:T(8,128)(2,1)S(1)} %collective-permute-done.1.far_ref, ...), custom_call_target="tpu_custom_call" | custom-call | tf_op jit(solution)/shard_map/column_kernel/pallas_call | solution.py:436
  42.2 0.0 all-to-all-done.2.row_ref
  42.2 0.0 copy-done.3
  42.2 0.9 %finish_kernel.1 = bf16[16,8,256]{2,1,0:T(8,128)(2,1)} custom-call(bf16[16,8,256]{2,1,0:T(8,128)(2,1)S(1)} %all-to-all-done.2.row_ref, f32[128,256]{1,0:T(8,128)S(1)} %get-tuple-element.28.col_ref, f32[128,256]{1,0:T(8,128)S(1)} %get-tuple-element.29.hidden_ref, f32[128,256]{1,0:T(8,128)S(1)} %get-tuple-element.30.gate_ref, ...), custom_call_target="tpu_custom_call" | custom-call | tf_op jit(solution)/shard_map/finish_kernel/pallas_call | solution.py:436
Async XLA Ops:
  17.0 13.3 %copy-start = (bf16[256,1024]{1,0:T(8,128)(2,1)S(1)}, bf16[256,1024]{1,0:T(8,128)(2,1)}, u32[]{:S(2)}) copy-start(bf16[256,1024]{1,0:T(8,128)(2,1)} %bc_ref.3) | copy-start | bytes 1572868
  17.7 12.6 %copy-start.1 = (bf16[256,512]{1,0:T(8,128)(2,1)S(1)}, bf16[256,512]{1,0:T(8,128)(2,1)}, u32[]{:S(2)}) copy-start(bf16[256,512]{1,0:T(8,128)(2,1)} %in_ref.3) | copy-start | bytes 786436
  17.7 12.6 %copy-start.2 = (bf16[256,64]{0,1:T(8,128)(2,1)S(1)}, bf16[256,64]{0,1:T(8,128)(2,1)}, u32[]{:S(2)}) copy-start(bf16[256,64]{0,1:T(8,128)(2,1)} %param.23) | copy-start | bytes 98308
  17.7 12.6 %copy-start.4 = (bf16[256,256]{1,0:T(8,128)(2,1)S(1)}, bf16[256,256]{1,0:T(8,128)(2,1)}, u32[]{:S(2)}) copy-start(bf16[256,256]{1,0:T(8,128)(2,1)} %cond_ref.1) | copy-start | bytes 393220
  17.7 12.5 %all-to-all-start.1 = ((bf16[16,8,1152]{2,1,0:T(8,128)(2,1)}), bf16[16,8,1152]{2,1,0:T(8,128)(2,1)S(1)}, u32[]{:S(2)}, u32[]{:S(2)}) async-start(bf16[16,8,1152]{2,1,0:T(8,128)(2,1)} %get-tuple-element.21), calls=%async_computation.1 | async-start | bytes 589824 | tf_op jit(solution)/shard_map/all_to_all | solution.py:499
  25.0 13.7 %collective-permute-start = (bf16[8,16,256]{2,1,0:T(8,128)(2,1)S(1)}, bf16[8,16,256]{2,1,0:T(8,128)(2,1)S(1)}, u32[]{:S(2)}, u32[]{:S(2)}) collective-permute-start(bf16[8,16,256]{2,1,0:T(8,128)(2,1)S(1)} %get-tuple-element.25), channel_id=1, source_target_pairs={{0,1},{1,0},{2,3},{3,2},{4,5},{5,4},{6,7},{7,6},{8,9},{9,8},{10,11... | collective-permute-start | bytes 196616 | tf_op jit(solution)/shard_map/ppermute | solution.py:496
  25.5 13.3 %collective-permute-start.1 = (bf16[8,16,256]{2,1,0:T(8,128)(2,1)S(1)}, bf16[8,16,256]{2,1,0:T(8,128)(2,1)S(1)}, u32[]{:S(2)}, u32[]{:S(2)}) collective-permute-start(bf16[8,16,256]{2,1,0:T(8,128)(2,1)S(1)} %get-tuple-element.26), channel_id=1, source_target_pairs={{1,2},{3,4},{5,6},{7,8},{9,10},{11,12},{13,14},{2,1},{4,3},{6,5},{... | collective-permute-start | bytes 196616 | tf_op jit(solution)/shard_map/ppermute | solution.py:498
  33.1 9.1 %all-to-all-start.2 = ((bf16[16,8,256]{2,1,0:T(8,128)(2,1)}), bf16[16,8,256]{2,1,0:T(8,128)(2,1)S(1)}, u32[]{:S(2)}, u32[]{:S(2)}) async-start(bf16[16,8,256]{2,1,0:T(8,128)(2,1)} %bitcast.4), calls=%async_computation.2 | async-start | bytes 131072 | tf_op jit(solution)/shard_map/all_to_all | solution.py:517
  38.7 3.5 %copy-start.3 = (bf16[256,256]{1,0:T(8,128)(2,1)S(1)}, bf16[256,256]{1,0:T(8,128)(2,1)}, u32[]{:S(2)}) copy-start(bf16[256,256]{1,0:T(8,128)(2,1)} %out_w_ref.1) | copy-start | bytes 393220
